TPU v7x, 32 devices: a whole 2x2x4 slice. The times are simulated.
32 devices in a mesh: tm: 8 (over z, x), rows: 4 (over y, core).
Axes of the slice: x: 2, y: 2, z: 4, core: 2. Of those that a mesh axis runs over, the one named last changes fastest.
Arguments:
- clip: float32 [32, 8, 32, 128], P('tm', 'rows'), may hold values from -6 to 6
- kernel_one: float32 [3, 3, 3, 128, 128], replicated, may hold values from -0.109375 to 0.109375
- kernel_two: float32 [3, 3, 3, 128, 128], replicated, may hold values from -0.109375 to 0.109375
- cotangent: float32 [32, 8, 32, 128], P('tm', 'rows'), may hold values from -6 to 6
Outputs:
- block_out: float32 [32, 8, 32, 128], P('tm', 'rows')
- grad_clip: float32 [32, 8, 32, 128], P('tm', 'rows')
- grad_one: float32 [3, 3, 3, 128, 128], replicated
- grad_two: float32 [3, 3, 3, 128, 128], replicated
All inputs are finite; a program needn't handle non-finite values.
Results may differ from a plain program's by a relative error of at most 0.00014.
Values sent between devices are 32-bit elements; how exact they have to be, the bound alone decides.
No kernel may reach another device: no remote copies, remote signals or barrier semaphores. Data moves between devices by JAX's collectives and lax.ppermute only.
A program may use at most 128 MiB of HBM per device.

v0:
```python
import math

import jax
import jax.numpy as jnp
from jax import lax
from jax.experimental import pallas as pl
from jax.experimental.pallas import tpu as pltpu
from jax.sharding import PartitionSpec as P

F32, BF16 = jnp.float32, jnp.bfloat16
VM, HBM = pltpu.VMEM, pltpu.HBM


def shaped(*dims, kind=F32):
    return jax.ShapeDtypeStruct(dims, kind)


def kernel(body, outs, args, scratch=(), flops=0, limit=20, far_in=(), far_out=(), alias=None):
    moved = sum(a.size * a.dtype.itemsize for a in (*args, *outs))
    args = [pltpu.with_memory_space_constraint(a, HBM) if i in far_in else a for i, a in enumerate(args)]
    return pl.pallas_call(
        body,
        out_shape=list(outs),
        in_specs=[pl.BlockSpec(memory_space=HBM if i in far_in else VM) for i in range(len(args))],
        out_specs=[pl.BlockSpec(memory_space=HBM if i in far_out else VM) for i in range(len(outs))],
        scratch_shapes=list(scratch),
        input_output_aliases=alias or {},
        compiler_params=pltpu.CompilerParams(vmem_limit_bytes=limit << 20),
        cost_estimate=pl.CostEstimate(flops=flops, bytes_accessed=moved, transcendentals=0),
    )(*args)


def halves(value):
    high = value.astype(BF16)
    return high, (value - high.astype(F32)).astype(BF16)


def moved_column(value, step, span):
    if step == 0:
        return value
    count = value.shape[0]
    column = lax.broadcasted_iota(jnp.int32, value.shape, 0) % span
    edge = span - 1 if step > 0 else 0
    return jnp.where(column == edge, 0.0, pltpu.roll(value, (-step) % count, 0))


def weights_body(plain, turned, *refs):
    count = (len(refs) - 4) // 2
    extra, (plain_out, turned_out), near = refs[:count], refs[count : count + 2], refs[count + 2 : -2]
    held, sem = refs[-2:]
    taps, ch = plain.shape[0], plain.shape[1]
    block = taps // 3
    copies = []
    for k in range(3):
        part = pl.ds(k * block, block)
        for which, source in enumerate((plain, turned)):
            copies.append(pltpu.make_async_copy(source.at[part], held.at[which, part], sem.at[which, k]))
    side = [pltpu.make_async_copy(a, b, sem.at[2, k]) for k, (a, b) in enumerate(zip(extra, near))]
    for copy in (*copies, *side):
        copy.start()

    def step(tap, carry):
        high, low = halves(held[0, tap])
        plain_out[tap, :, 0:ch] = high
        plain_out[tap, :, ch : 2 * ch] = low
        high, low = halves(held[1, tap].T)
        turned_out[taps - 1 - tap, :, 0:ch] = high
        turned_out[taps - 1 - tap, :, ch : 2 * ch] = low
        return carry

    for k in range(3):
        copies[2 * k].wait()
        copies[2 * k + 1].wait()
        lax.fori_loop(k * block, (k + 1) * block, step, 0, unroll=True)
    for copy in side:
        copy.wait()


def weights(plain, turned, extra):
    taps, ch = plain.shape[0], plain.shape[1]
    out = shaped(taps, ch, 2 * ch, kind=BF16)
    return kernel(
        weights_body,
        [out, out, *(shaped(*v.shape) for v in extra)],
        (plain, turned, *extra),
        scratch=[pltpu.VMEM((2, taps, ch, ch), F32), pltpu.SemaphoreType.DMA((3, 3))],
        far_in=range(2 + len(extra)),
    )


def ends_body(first, second, tail, head, sem):
    frames, depth = first.shape[0], tail.shape[0]
    one = pltpu.make_async_copy(first.at[pl.ds(frames - depth, depth)], tail, sem.at[0])
    two = pltpu.make_async_copy(second.at[pl.ds(0, depth)], head, sem.at[1])
    one.start()
    two.start()
    one.wait()
    two.wait()


def pack_body(first, second, before, after, whole, outer, inner=None):
    frames = first.shape[0]
    depth = whole.shape[1] - frames
    lead = before.shape[0] - depth
    rows = first.shape[1]
    odd = lax.axis_index("rows") % 2
    whole[0, depth:] = first[...]
    whole[0, 0:depth] = before[lead:]
    whole[1, 0:frames] = second[...]
    whole[1, frames:] = after[0:depth]
    outer[...] = whole[:, :, odd * (rows - 1)]
    if inner is not None:
        inner[...] = whole[:, :, (1 - odd) * (rows - 1)]


def pack(first, second, before, after, edges):
    frames, rows, span, ch = first.shape
    edge = shaped(2, frames + 2, span, ch)
    return kernel(pack_body, [shaped(2, frames + 2, rows, span, ch)] + [edge] * edges, (first, second, before, after))


def convolve(strip, weight, shifted, columns):
    tall, wide, span, ch = strip.shape
    frames, rows = tall - 2, wide - 2
    cells = frames * rows * span
    flat = strip[...].reshape(tall * wide * span, ch)
    for c in range(3):
        high, low = halves(moved_column(flat, c - 1, span))
        shifted[0, c] = high.reshape(tall, wide, span, ch)
        shifted[1, c] = low.reshape(tall, wide, span, ch)
    for part in range(2):
        for a in range(3):
            for b in range(3):
                for c in range(3):
                    tap = (a * 3 + b) * 3 + c
                    piece = shifted[part, c, a : a + frames, b : b + rows]
                    columns[part, :, tap * ch : (tap + 1) * ch] = piece.reshape(cells, ch)
    matrix = weight[...].reshape(27 * ch, 2 * ch)
    main = jnp.dot(columns[0], matrix, preferred_element_type=F32)
    rest = jnp.dot(columns[1], matrix[:, :ch], preferred_element_type=F32)
    return main[:, :ch] + main[:, ch:] + rest


def conv_scratch(frames, rows, span, ch):
    return [
        pltpu.VMEM((frames + 2, rows + 2, span, ch), F32),
        pltpu.VMEM((2, 3, frames + 2, rows + 2, span, ch), BF16),
        pltpu.VMEM((2, frames * rows * span, 27 * ch), BF16),
    ]


def place_rows(strip, own, outer, inner, odd):
    rows = own.shape[1]
    strip[:, 1 : rows + 1] = own
    strip[:, odd * (rows + 1)] = outer
    strip[:, (1 - odd) * (rows + 1)] = inner


def forward_body(own, partner, outer, w_one, w_two, active, delta, tail, head, crossing, strip, shifted, columns):
    odd = lax.axis_index("rows") % 2
    rows = own.shape[2]
    near = odd * (rows - 1)
    place_rows(strip, own[0], outer[0], partner[0, :, near], odd)
    pre = convolve(strip, w_one, shifted, columns)
    place_rows(strip, own[1], outer[1], partner[1, :, near], odd)
    slope = convolve(strip, w_two, shifted, columns)
    gate = jax.nn.sigmoid(pre)
    act = (pre * gate).reshape(active.shape)
    dlt = (slope * gate * (1.0 + pre * (1.0 - gate))).reshape(delta.shape)
    active[...] = act
    delta[...] = dlt
    tail[...] = act[active.shape[0] - 2 :]
    head[...] = dlt[:2]
    crossing[...] = jnp.where(odd == 0, dlt, act)


def outputs_body(ext, outer, inner, w_two, w_one, clip, cotangent, block_out, grad_clip, strip, shifted, columns):
    odd = lax.axis_index("rows") % 2
    place_rows(strip, ext[0], outer[0], inner[0], odd)
    block_out[...] = clip[...] + convolve(strip, w_two, shifted, columns).reshape(clip.shape)
    place_rows(strip, ext[1], outer[1], inner[1], odd)
    grad_clip[...] = cotangent[...] + convolve(strip, w_one, shifted, columns).reshape(clip.shape)


def grads_body(sending, own, partner, outer, far, active, delta, arrived, first, second, field, wide, turned):
    odd = lax.axis_index("rows") % 2
    y_bit = (lax.axis_index("rows") // 2) % 2
    x_bit = lax.axis_index("tm") % 2
    tall, rows, span, ch = own.shape[1:]
    frames = active.shape[0]
    pick = 1 - odd
    field[:, pl.ds(1 + rows * odd, rows)] = own[pick]
    field[:, pl.ds(1 + rows * (1 - odd), rows)] = partner[pick]
    field[:, odd * (2 * rows + 1)] = outer[pick]
    field[:, (1 - odd) * (2 * rows + 1)] = far[pick]
    flat = field[...].reshape(tall * (2 * rows + 2) * span, ch)
    for c in range(3):
        high, low = halves(moved_column(flat, c - 1, span))
        wide[c, :, :, :, 0:ch] = high.reshape(field.shape)
        wide[c, :, :, :, ch : 2 * ch] = low.reshape(field.shape)
    mine = jnp.where(odd == 0, active[...], delta[...])
    other = arrived[...]
    swap = odd == 1
    upper = jnp.where(swap, other, mine)
    lower = jnp.where(swap, mine, other)
    cells = frames * 2 * rows * span
    joined = jnp.concatenate([upper, lower], 1).reshape(cells, ch).T
    high, low = halves(joined)
    turned[0:ch] = high
    turned[ch : 2 * ch] = low

    def tap_of(group, j):
        tap = jnp.minimum(group * 7 + j, 26)
        a, b, c = tap // 9, (tap // 3) % 3, tap % 3
        piece = wide[c, pl.ds(a, frames), pl.ds(b, 2 * rows)].reshape(cells, 2 * ch)
        product = jnp.dot(turned[...], piece, preferred_element_type=F32)
        left = product[:, :ch] + product[:, ch:]
        return left[:ch] + left[ch:]

    def step(j, carry):
        first[j] = tap_of(y_bit ^ sending, j)
        second[j] = tap_of(2 + (x_bit ^ sending), j)
        return carry

    lax.fori_loop(0, 7, step, 0, unroll=True)


def grads(sending, own, partner, outer, far, active, delta, arrived):
    frames, rows, span, ch = active.shape
    out = shaped(7, ch, ch)
    field = (frames + 2, 2 * rows + 2, span, ch)
    return kernel(
        lambda *refs: grads_body(sending, *refs),
        [out, out],
        (own, partner, outer, far, active, delta, arrived),
        scratch=[
            pltpu.VMEM(field, F32),
            pltpu.VMEM((3, *field[:-1], 2 * ch), BF16),
            pltpu.VMEM((2 * ch, frames * 2 * rows * span), BF16),
        ],
        flops=14 * 2 * (2 * ch) ** 2 * frames * 2 * rows * span,
    )


def halve_body(keep_a, keep_b, got_a, got_b, stay_a, go_a, stay_b, go_b):
    x_bit = lax.axis_index("tm") % 2
    y_bit = (lax.axis_index("rows") // 2) % 2
    half = stay_a.shape[0]
    for keep, got, bit, stay, go in ((keep_a, got_a, x_bit, stay_a, go_a), (keep_b, got_b, y_bit, stay_b, go_b)):
        near = pl.ds(pl.multiple_of(bit * half, 8), half)
        away = pl.ds(pl.multiple_of((1 - bit) * half, 8), half)
        go[...] = keep[away] + got[away]
        stay[...] = keep[near] + got[near]


def quarter_body(keep_a, keep_b, got_a, got_b, *outs):
    z = (lax.axis_index("tm") // 2) % 4
    size = outs[0].shape[1]
    for d in range(4):
        part = pl.ds(pl.multiple_of((z ^ d) * size, 8), size)
        outs[d][0] = keep_a[part] + got_a[part]
        outs[d][1] = keep_b[part] + got_b[part]


def total_body(factor, *refs):
    *parts, out = refs
    value = parts[0][...]
    for part in parts[1:]:
        value = value + part[...]
    out[...] = value * factor


def join_quarters_body(q0, q1, q2, q3, out_a, out_b):
    z = (lax.axis_index("tm") // 2) % 4
    size = q0.shape[1]
    for d, quarter in enumerate((q0, q1, q2, q3)):
        part = pl.ds(pl.multiple_of((z ^ d) * size, 8), size)
        out_a[part] = quarter[0]
        out_b[part] = quarter[1]


def join_halves_body(own_a, got_a, own_b, got_b, out_a, out_b):
    x_bit = lax.axis_index("tm") % 2
    y_bit = (lax.axis_index("rows") // 2) % 2
    half = own_a.shape[0]
    for own, got, bit, out in ((own_a, got_a, x_bit, out_a), (own_b, got_b, y_bit, out_b)):
        out[pl.ds(pl.multiple_of(bit * half, 8), half)] = own[...]
        out[pl.ds(pl.multiple_of((1 - bit) * half, 8), half)] = got[...]


def finish_body(late, *refs):
    mine, other = refs[0:2], refs[2:4]
    one, two, turned, sem = refs[-4:]
    odd = lax.axis_index("rows") % 2
    x_bit = lax.axis_index("tm") % 2
    y_bit = (lax.axis_index("rows") // 2) % 2
    groups = (y_bit ^ late, 2 + (x_bit ^ late))
    spots = [(k, j) for k in range(2) for j in range(7)]

    def plain(k, j, source):
        return pltpu.make_async_copy(source.at[j], two.at[26 - (groups[k] * 7 + j)], sem.at[0, k, j])

    def flipped(k, j):
        return pltpu.make_async_copy(turned.at[k, j], one.at[groups[k] * 7 + j], sem.at[1, k, j])

    for k, j in spots:
        inside = groups[k] * 7 + j < 27

        @pl.when(inside & (odd == 0))
        def _():
            plain(k, j, mine[k]).start()

        @pl.when(inside & (odd == 1))
        def _():
            plain(k, j, other[k]).start()

    for k in range(2):
        for j in range(7):
            turned[k, j] = jnp.where(odd == 0, other[k][j], mine[k][j]).T
    for start in (True, False):
        for k, j in spots:

            @pl.when(groups[k] * 7 + j < 27)
            def _():
                if start:
                    flipped(k, j).start()
                else:
                    plain(k, j, mine[k]).wait()
                    flipped(k, j).wait()


def finish(late, mine, other, grads_so_far):
    ch = mine[0].shape[-1]
    grad = shaped(27, ch, ch)
    args = [v.reshape(7, ch, ch) for v in (*mine, *other)] + list(grads_so_far)
    return list(kernel(
        lambda *refs: finish_body(late, *refs),
        [grad, grad],
        args,
        scratch=[pltpu.VMEM((2, 7, ch, ch), F32), pltpu.SemaphoreType.DMA((2, 2, 7))],
        far_in=(4, 5),
        far_out=(0, 1),
        alias={4: 0, 5: 1} if grads_so_far else None,
    ))


def tied(*values):
    return list(lax.optimization_barrier(values))


def swapped(value, axis, bits):
    return lax.ppermute(value, axis, [(i, i ^ bits) for i in range(lax.axis_size(axis))])


def per_device(clip, kernel_one, kernel_two, cotangent):
    frames, rows, span, ch = clip.shape
    tm, strips = lax.axis_size("tm"), lax.axis_size("rows")
    factor = 1.0 / math.sqrt(frames * tm * rows * strips * span)
    later = [(i, i + 1) for i in range(tm - 1)]
    earlier = [(i + 1, i) for i in range(tm - 1)]
    across = [pair for i in range(1, strips - 1, 2) for pair in ((i, i + 1), (i + 1, i))]

    strip = shaped(2, rows, span, ch)
    tail, head = kernel(
        ends_body, [strip, strip], (clip, cotangent), scratch=[pltpu.SemaphoreType.DMA((2,))], far_in=(0, 1)
    )
    before = lax.ppermute(tail, "tm", later)
    after = lax.ppermute(head, "tm", earlier)
    one, two = kernel_one.reshape(27, ch, ch), kernel_two.reshape(27, ch, ch)
    one_plain, two_turned, clip_near, cot_near = weights(one, two, (clip, cotangent))
    before, after, one_plain, two_turned = tied(before, after, one_plain, two_turned)
    own, edge = pack(clip_near, cot_near, before, after, 1)
    outer = lax.ppermute(edge, "rows", across)
    partner = swapped(own, "rows", 1)
    far = swapped(outer, "rows", 1)

    cell = shaped(frames, rows, span, ch)
    conv_flops = 3 * 2 * frames * rows * span * 27 * ch * ch
    active, delta, tail, head, crossing = kernel(
        forward_body,
        [cell, cell, strip, strip, cell],
        (own, partner, outer, one_plain, two_turned),
        scratch=conv_scratch(frames, rows, span, ch),
        flops=2 * conv_flops,
    )
    arrived = swapped(crossing, "rows", 1)

    shared = (own, partner, outer, far, active, delta, arrived)
    give_a, give_b = grads(1, *shared)
    got_a = swapped(give_a, "rows", 2)
    got_b = swapped(give_b, "tm", 1)
    keep_a, keep_b = grads(0, *shared)
    keep_a, one, two = tied(keep_a, one, two)
    two_plain, one_turned = weights(two, one, ())
    keep_a, two_plain, one_turned = tied(keep_a, two_plain, one_turned)

    size = 7 * ch
    half = shaped(size // 2, ch)
    stay_a, go_a, stay_b, go_b = kernel(
        halve_body, [half] * 4, tuple(v.reshape(size, ch) for v in (keep_a, keep_b, got_a, got_b))
    )
    got_a = swapped(go_a, "tm", 1)
    got_b = swapped(go_b, "rows", 2)
    quarter = shaped(2, size // 8, ch)
    parts = list(kernel(quarter_body, [quarter] * 4, (stay_a, stay_b, got_a, got_b)))
    summed = [parts[0]] + [swapped(parts[d], "tm", 2 * d) for d in range(1, 4)]

    before = lax.ppermute(tail, "tm", later)
    after = lax.ppermute(head, "tm", earlier)
    ext, edge, inside = pack(active, delta, before, after, 2)

    wider = [("tm", 1 << k) for k in range(3, tm.bit_length() - 1)]
    wider += [("rows", 1 << k) for k in range(2, strips.bit_length() - 1)]
    for axis, bits in wider:
        (shard,) = kernel(lambda *refs: total_body(1.0, *refs), [quarter], summed)
        summed = [shard, swapped(shard, axis, bits)]
    (shard,) = kernel(lambda *refs: total_body(factor, *refs), [quarter], summed)

    quarters = [shard] + [swapped(shard, "tm", 2 * d) for d in range(1, 4)]
    outer = lax.ppermute(edge, "rows", across)
    inner = swapped(inside, "rows", 1)
    own_a, own_b = kernel(join_quarters_body, [half] * 2, quarters)
    got_a = swapped(own_a, "tm", 1)
    got_b = swapped(own_b, "rows", 2)
    full = shaped(size, ch)
    mine = kernel(join_halves_body, [full] * 2, (own_a, got_a, own_b, got_b))
    got = [swapped(mine[0], "rows", 2), swapped(mine[1], "tm", 1)]
    other = [swapped(v, "rows", 1) for v in mine]
    half_done = finish(0, mine, other, ())
    half_done[0], outer, inner = tied(half_done[0], outer, inner)
    block_out, grad_clip = kernel(
        outputs_body,
        [cell, cell],
        (ext, outer, inner, two_plain, one_turned, clip, cotangent),
        scratch=conv_scratch(frames, rows, span, ch),
        flops=2 * conv_flops,
    )
    got[0], got[1], block_out, grad_clip = tied(*got, block_out, grad_clip)
    got_other = [swapped(v, "rows", 1) for v in got]
    grad_one, grad_two = finish(1, got, got_other, half_done)
    shape = kernel_one.shape
    return block_out, grad_clip, grad_one.reshape(shape), grad_two.reshape(shape)


def solution(mesh):
    return jax.shard_map(
        per_device,
        mesh=mesh,
        in_specs=(P("tm", "rows", None, None), P(), P(), P("tm", "rows", None, None)),
        out_specs=(P("tm", "rows", None, None), P("tm", "rows", None, None), P(), P()),
        check_vma=False,
    )
```

profile of v0, /device:TPU:0, one launch (start us, length us, event | category | flops | bytes accessed | tf_op | source)
XLA Modules:
  0.0 115.1 jit_solution(15930034889219399695)
XLA Ops:
  1.5 4.9 %collective-permute-start = (f32[2,2,32,128]{3,2,1,0:T(8,128)S(1)}, f32[2,2,32,128]{3,2,1,0:T(8,128)S(1)}, u32[]{:S(2)}, u32[]{:S(2)}) collective-permute-start(f32[2,2,32,128]{3,2,1,0:T(8,128)S(1)} %get-tuple-element.63), channel_id=1, source_target_pairs={{0,4},{4,8},{8,12},{12,16},{16,20},{20,24},{24,28},{1,5},{5,9},{9,... | collective-permute-start | bytes 196616 | tf_op jit(solution)/shard_map/ppermute | solution.py:367
  7.7 2.3 %shard_map.75 = (bf16[27,128,256]{2,1,0:T(8,128)(2,1)S(1)}, bf16[27,128,256]{2,1,0:T(8,128)(2,1)S(1)}, f32[4,2,32,128]{3,2,1,0:T(8,128)S(1)}, f32[4,2,32,128]{3,2,1,0:T(8,128)S(1)}) custom-call(f32[27,128,128]{2,1,0:T(8,128)} %bitcast.28, f32[27,128,128]{2,1,0:T(8,128)} %bitcast.30, f32[4,2,32,128]{3,2,1,0:T(8,128)} %clip.1, f32[4,2,32,128]{3,2,1,0:T(8,128)} %cotangent.1), custom_call_target="tpu_custom_call" | custom-call | bytes 7602176 | tf_op jit(solution)/shard_map/pallas_call | solution.py:21
  10.0 2.5 %collective-permute-done.1.after = f32[2,2,32,128]{3,2,1,0:T(8,128)S(1)} collective-permute-done((f32[2,2,32,128]{3,2,1,0:T(8,128)S(1)}, f32[2,2,32,128]{3,2,1,0:T(8,128)S(1)}, u32[]{:S(2)}, u32[]{:S(2)}) %collective-permute-start.1) | collective-permute-done | bytes 65568 | tf_op jit(solution)/shard_map/ppermute | solution.py:368
  13.4 6.8 %collective-permute-start.4 = (f32[2,6,32,128]{3,2,1,0:T(8,128)S(1)}, f32[2,6,32,128]{3,2,1,0:T(8,128)S(1)}, u32[]{:S(2)}, u32[]{:S(2)}) collective-permute-start(f32[2,6,32,128]{3,2,1,0:T(8,128)S(1)} %collective-permute-done.3.outer.refs_2_), channel_id=1, source_target_pairs={{0,1},{1,0},{2,3},{3,2},{4,5},{5,4},{6,7},{7,6},{8,9},{9,8},{10,11... | collective-permute-start | bytes 589832 | tf_op jit(solution)/shard_map/ppermute | solution.py:352
  20.2 3.0 %shard_map.78 = (f32[4,2,32,128]{3,2,1,0:T(8,128)S(1)}, f32[4,2,32,128]{3,2,1,0:T(8,128)S(1)}, f32[2,2,32,128]{3,2,1,0:T(8,128)S(1)}, f32[2,2,32,128]{3,2,1,0:T(8,128)S(1)}, f32[4,2,32,128]{3,2,1,0:T(8,128)S(1)}) custom-call(f32[2,6,2,32,128]{4,3,2,1,0:T(8,128)S(1)} %get-tuple-element.69.own.refs_0_, ...), custom_call_target="tpu_custom_call" | custom-call | flops 1358954496 | bytes 5046272 | tf_op jit(solution)/shard_map/pallas_call | solution.py:21
  23.2 1.3 %collective-permute-done.5.refs_6_ = f32[4,2,32,128]{3,2,1,0:T(8,128)S(1)} collective-permute-done((f32[4,2,32,128]{3,2,1,0:T(8,128)S(1)}, f32[4,2,32,128]{3,2,1,0:T(8,128)S(1)}, u32[]{:S(2)}, u32[]{:S(2)}) %collective-permute-start.5) | collective-permute-done | bytes 131104 | tf_op jit(solution)/shard_map/ppermute | solution.py:352
  24.6 1.8 %shard_map.81 = (f32[7,128,128]{2,1,0:T(8,128)S(1)}, f32[7,128,128]{2,1,0:T(8,128)S(1)}) custom-call(f32[2,6,2,32,128]{4,3,2,1,0:T(8,128)S(1)} %get-tuple-element.69.own.refs_0_, f32[2,6,2,32,128]{4,3,2,1,0:T(8,128)S(1)} %collective-permute-done.2.partner.refs_1_, f32[2,6,32,128]{3,2,1,0:T(8,128)S(1)} %collective-permute-done.3.outer.refs_2_, ...), custom_call_target="tpu_custom_call" | custom-call | flops 939524096 | bytes 2490368 | tf_op jit(solution)/shard_map/pallas_call | solution.py:21
  27.6 2.4 %collective-permute-start.7 = (f32[7,128,128]{2,1,0:T(8,128)S(1)}, f32[7,128,128]{2,1,0:T(8,128)S(1)}, u32[]{:S(2)}, u32[]{:S(2)}) collective-permute-start(f32[7,128,128]{2,1,0:T(8,128)S(1)} %get-tuple-element.85), channel_id=1, source_target_pairs={{0,4},{4,0},{8,12},{12,8},{16,20},{20,16},{24,28},{28,24},{1,5},{5... | collective-permute-start | bytes 1376264 | tf_op jit(solution)/shard_map/ppermute | solution.py:352
  30.1 1.8 %shard_map.79 = (f32[7,128,128]{2,1,0:T(8,128)S(1)}, f32[7,128,128]{2,1,0:T(8,128)S(1)}) custom-call(f32[2,6,2,32,128]{4,3,2,1,0:T(8,128)S(1)} %get-tuple-element.69.own.refs_0_, f32[2,6,2,32,128]{4,3,2,1,0:T(8,128)S(1)} %collective-permute-done.2.partner.refs_1_, f32[2,6,32,128]{3,2,1,0:T(8,128)S(1)} %collective-permute-done.3.outer.refs_2_, ...), custom_call_target="tpu_custom_call" | custom-call | flops 939524096 | bytes 2490368 | tf_op jit(solution)/shard_map/pallas_call | solution.py:21
  31.9 2.3 %shard_map.80 = (bf16[27,128,256]{2,1,0:T(8,128)(2,1)S(1)}, bf16[27,128,256]{2,1,0:T(8,128)(2,1)S(1)}) custom-call(f32[27,128,128]{2,1,0:T(8,128)} %bitcast.31, f32[27,128,128]{2,1,0:T(8,128)} %bitcast.29), custom_call_target="tpu_custom_call" | custom-call | bytes 7077888 | tf_op jit(solution)/shard_map/pallas_call | solution.py:21
  34.2 4.8 %collective-permute-done.6 = f32[7,128,128]{2,1,0:T(8,128)S(1)} collective-permute-done((f32[7,128,128]{2,1,0:T(8,128)S(1)}, f32[7,128,128]{2,1,0:T(8,128)S(1)}, u32[]{:S(2)}, u32[]{:S(2)}) %collective-permute-start.6) | collective-permute-done | bytes 458784 | tf_op jit(solution)/shard_map/ppermute | solution.py:352
  39.0 1.8 %collective-permute-done.7 = f32[7,128,128]{2,1,0:T(8,128)S(1)} collective-permute-done((f32[7,128,128]{2,1,0:T(8,128)S(1)}, f32[7,128,128]{2,1,0:T(8,128)S(1)}, u32[]{:S(2)}, u32[]{:S(2)}) %collective-permute-start.7) | collective-permute-done | bytes 458784 | tf_op jit(solution)/shard_map/ppermute | solution.py:352
  41.0 1.8 %collective-permute-start.8 = (f32[448,128]{1,0:T(8,128)S(1)}, f32[448,128]{1,0:T(8,128)S(1)}, u32[]{:S(2)}, u32[]{:S(2)}) collective-permute-start(f32[448,128]{1,0:T(8,128)S(1)} %get-tuple-element.88), channel_id=1, source_target_pairs={{0,4},{4,0},{8,12},{12,8},{16,20},{20,16},{24,28},{28,24},{1,5},{5... | collective-permute-start | bytes 688136 | tf_op jit(solution)/shard_map/ppermute | solution.py:352
  43.4 4.7 %collective-permute-done.8.got_a = f32[448,128]{1,0:T(8,128)S(1)} collective-permute-done((f32[448,128]{1,0:T(8,128)S(1)}, f32[448,128]{1,0:T(8,128)S(1)}, u32[]{:S(2)}, u32[]{:S(2)}) %collective-permute-start.8) | collective-permute-done | bytes 229408 | tf_op jit(solution)/shard_map/ppermute | solution.py:352
  49.3 1.6 %collective-permute-start.10 = (f32[2,112,128]{2,1,0:T(8,128)S(1)}, f32[2,112,128]{2,1,0:T(8,128)S(1)}, u32[]{:S(2)}, u32[]{:S(2)}) collective-permute-start(f32[2,112,128]{2,1,0:T(8,128)S(1)} %get-tuple-element.91), channel_id=1, source_target_pairs={{0,8},{4,12},{8,0},{12,4},{16,24},{20,28},{24,16},{28,20},{1,9},{5... | collective-permute-start | bytes 344072 | tf_op jit(solution)/shard_map/ppermute | solution.py:352
  52.0 1.7 %collective-permute-start.12 = (f32[2,112,128]{2,1,0:T(8,128)S(1)}, f32[2,112,128]{2,1,0:T(8,128)S(1)}, u32[]{:S(2)}, u32[]{:S(2)}) collective-permute-start(f32[2,112,128]{2,1,0:T(8,128)S(1)} %get-tuple-element.93), channel_id=1, source_target_pairs={{0,24},{4,28},{8,16},{12,20},{16,8},{20,12},{24,0},{28,4},{1,25},{... | collective-permute-start | bytes 344072 | tf_op jit(solution)/shard_map/ppermute | solution.py:352
  54.6 6.2 %collective-permute-done.11.refs_2_ = f32[2,112,128]{2,1,0:T(8,128)S(1)} collective-permute-done((f32[2,112,128]{2,1,0:T(8,128)S(1)}, f32[2,112,128]{2,1,0:T(8,128)S(1)}, u32[]{:S(2)}, u32[]{:S(2)}) %collective-permute-start.11) | collective-permute-done | bytes 114720 | tf_op jit(solution)/shard_map/ppermute | solution.py:352
  60.9 1.9 %collective-permute-start.13 = (f32[2,112,128]{2,1,0:T(8,128)S(1)}, f32[2,112,128]{2,1,0:T(8,128)S(1)}, u32[]{:S(2)}, u32[]{:S(2)}) collective-permute-start(f32[2,112,128]{2,1,0:T(8,128)S(1)} %shard_map.84.q0), channel_id=1, source_target_pairs={{0,8},{4,12},{8,0},{12,4},{16,24},{20,28},{24,16},{28,20},{1,9},{5... | collective-permute-start | bytes 344072 | tf_op jit(solution)/shard_map/ppermute | solution.py:352
  63.8 1.5 %collective-permute-start.15 = (f32[2,112,128]{2,1,0:T(8,128)S(1)}, f32[2,112,128]{2,1,0:T(8,128)S(1)}, u32[]{:S(2)}, u32[]{:S(2)}) collective-permute-start(f32[2,112,128]{2,1,0:T(8,128)S(1)} %shard_map.84.q0), channel_id=1, source_target_pairs={{0,24},{4,28},{8,16},{12,20},{16,8},{20,12},{24,0},{28,4},{1,25},{... | collective-permute-start | bytes 344072 | tf_op jit(solution)/shard_map/ppermute | solution.py:352
  65.4 1.6 %collective-permute-done.13.q1 = f32[2,112,128]{2,1,0:T(8,128)S(1)} collective-permute-done((f32[2,112,128]{2,1,0:T(8,128)S(1)}, f32[2,112,128]{2,1,0:T(8,128)S(1)}, u32[]{:S(2)}, u32[]{:S(2)}) %collective-permute-start.13) | collective-permute-done | bytes 114720 | tf_op jit(solution)/shard_map/ppermute | solution.py:352
  66.9 6.8 %collective-permute-done.14.q2 = f32[2,112,128]{2,1,0:T(8,128)S(1)} collective-permute-done((f32[2,112,128]{2,1,0:T(8,128)S(1)}, f32[2,112,128]{2,1,0:T(8,128)S(1)}, u32[]{:S(2)}, u32[]{:S(2)}) %collective-permute-start.14) | collective-permute-done | bytes 114720 | tf_op jit(solution)/shard_map/ppermute | solution.py:352
  74.9 4.9 %collective-permute-done.16.got_a = f32[448,128]{1,0:T(8,128)S(1)} collective-permute-done((f32[448,128]{1,0:T(8,128)S(1)}, f32[448,128]{1,0:T(8,128)S(1)}, u32[]{:S(2)}, u32[]{:S(2)}) %collective-permute-start.16) | collective-permute-done | bytes 229408 | tf_op jit(solution)/shard_map/ppermute | solution.py:352
  81.6 1.4 %collective-permute-start.19 = (f32[896,128]{1,0:T(8,128)S(1)}, f32[896,128]{1,0:T(8,128)S(1)}, u32[]{:S(2)}, u32[]{:S(2)}) collective-permute-start(f32[896,128]{1,0:T(8,128)S(1)} %get-tuple-element.97), channel_id=1, source_target_pairs={{0,4},{4,0},{8,12},{12,8},{16,20},{20,16},{24,28},{28,24},{1,5},{5... | collective-permute-start | bytes 1376264 | tf_op jit(solution)/shard_map/ppermute | solution.py:352
  83.1 2.5 %collective-permute-start.20 = (f32[2,2,32,128]{3,2,1,0:T(8,128)S(1)}, f32[2,2,32,128]{3,2,1,0:T(8,128)S(1)}, u32[]{:S(2)}, u32[]{:S(2)}) collective-permute-start(f32[2,2,32,128]{3,2,1,0:T(8,128)S(1)} %get-tuple-element.98), channel_id=1, source_target_pairs={{0,4},{4,8},{8,12},{12,16},{16,20},{20,24},{24,28},{1,5},{5,9},{9,... | collective-permute-start | bytes 196616 | tf_op jit(solution)/shard_map/ppermute | solution.py:408
  85.6 8.7 %collective-permute-done.20.before = f32[2,2,32,128]{3,2,1,0:T(8,128)S(1)} collective-permute-done((f32[2,2,32,128]{3,2,1,0:T(8,128)S(1)}, f32[2,2,32,128]{3,2,1,0:T(8,128)S(1)}, u32[]{:S(2)}, u32[]{:S(2)}) %collective-permute-start.20) | collective-permute-done | bytes 65568 | tf_op jit(solution)/shard_map/ppermute | solution.py:408
  95.5 5.3 %collective-permute-done.21.after = f32[2,2,32,128]{3,2,1,0:T(8,128)S(1)} collective-permute-done((f32[2,2,32,128]{3,2,1,0:T(8,128)S(1)}, f32[2,2,32,128]{3,2,1,0:T(8,128)S(1)}, u32[]{:S(2)}, u32[]{:S(2)}) %collective-permute-start.21) | collective-permute-done | bytes 65568 | tf_op jit(solution)/shard_map/ppermute | solution.py:409
  101.8 2.9 %collective-permute-start.25 = (f32[2,6,32,128]{3,2,1,0:T(8,128)S(1)}, f32[2,6,32,128]{3,2,1,0:T(8,128)S(1)}, u32[]{:S(2)}, u32[]{:S(2)}) collective-permute-start(f32[2,6,32,128]{3,2,1,0:T(8,128)S(1)} %get-tuple-element.103), channel_id=1, source_target_pairs={{0,1},{1,0},{2,3},{3,2},{4,5},{5,4},{6,7},{7,6},{8,9},{9,8},{10,11... | collective-permute-start | bytes 589832 | tf_op jit(solution)/shard_map/ppermute | solution.py:352
  104.7 1.5 %shard_map.88 = (f32[27,128,128]{2,1,0:T(8,128)}, f32[27,128,128]{2,1,0:T(8,128)}) custom-call(f32[7,128,128]{2,1,0:T(8,128)S(1)} %bitcast.17, f32[7,128,128]{2,1,0:T(8,128)S(1)} %bitcast.16, f32[7,128,128]{2,1,0:T(8,128)S(1)} %bitcast.18, f32[7,128,128]{2,1,0:T(8,128)S(1)} %bitcast.19), custom_call_target="tpu_custom_call" | custom-call | bytes 5373952 | tf_op jit(solution)/shard_map/pallas_call | solution.py:21
  106.2 3.6 %shard_map.89 = (f32[4,2,32,128]{3,2,1,0:T(8,128)}, f32[4,2,32,128]{3,2,1,0:T(8,128)}) custom-call(f32[2,6,2,32,128]{4,3,2,1,0:T(8,128)S(1)} %get-tuple-element.100.ext, f32[2,6,32,128]{3,2,1,0:T(8,128)S(1)} %collective-permute-done.24.outer, f32[2,6,32,128]{3,2,1,0:T(8,128)S(1)} %collective-permute-done.25.inner, ...), custom_call_target="tpu_custom_call" | custom-call | flops 1358954496 | bytes 4849664 | tf_op jit(solution)/shard_map/pallas_call | solution.py:21
  109.9 1.6 %collective-permute-start.26 = (f32[896,128]{1,0:T(8,128)S(1)}, f32[896,128]{1,0:T(8,128)S(1)}, u32[]{:S(2)}, u32[]{:S(2)}) collective-permute-start(f32[896,128]{1,0:T(8,128)S(1)} %collective-permute-done.18), channel_id=1, source_target_pairs={{0,1},{1,0},{2,3},{3,2},{4,5},{5,4},{6,7},{7,6},{8,9},{9,8},{10,11... | collective-permute-start | bytes 1376264 | tf_op jit(solution)/shard_map/ppermute | solution.py:352
  111.5 1.4 %collective-permute-done.26 = f32[896,128]{1,0:T(8,128)S(1)} collective-permute-done((f32[896,128]{1,0:T(8,128)S(1)}, f32[896,128]{1,0:T(8,128)S(1)}, u32[]{:S(2)}, u32[]{:S(2)}) %collective-permute-start.26) | collective-permute-done | bytes 458784 | tf_op jit(solution)/shard_map/ppermute | solution.py:352
  113.5 1.4 %shard_map.90 = (f32[27,128,128]{2,1,0:T(8,128)}, f32[27,128,128]{2,1,0:T(8,128)}) custom-call(f32[7,128,128]{2,1,0:T(8,128)S(1)} %bitcast.24, f32[7,128,128]{2,1,0:T(8,128)S(1)} %bitcast.25, f32[7,128,128]{2,1,0:T(8,128)S(1)} %bitcast.26, f32[7,128,128]{2,1,0:T(8,128)S(1)} %bitcast.27, ...), custom_call_target="tpu_custom_call", output_to_operand_aliasing={{0}: (4, {}), {1}: (5, {})} | custom-call | bytes 8912896 | tf_op jit(solution)/shard_map/pallas_call | solution.py:21
  (44 shorter events, 15.2 us)
Async XLA Ops:
  1.5 8.5 %collective-permute-start = (f32[2,2,32,128]{3,2,1,0:T(8,128)S(1)}, f32[2,2,32,128]{3,2,1,0:T(8,128)S(1)}, u32[]{:S(2)}, u32[]{:S(2)}) collective-permute-start(f32[2,2,32,128]{3,2,1,0:T(8,128)S(1)} %get-tuple-element.63), channel_id=1, source_target_pairs={{0,4},{4,8},{8,12},{12,16},{16,20},{20,24},{24,28},{1,5},{5,9},{9,... | collective-permute-start | bytes 196616 | tf_op jit(solution)/shard_map/ppermute | solution.py:367
  6.4 6.2 %collective-permute-start.1 = (f32[2,2,32,128]{3,2,1,0:T(8,128)S(1)}, f32[2,2,32,128]{3,2,1,0:T(8,128)S(1)}, u32[]{:S(2)}, u32[]{:S(2)}) collective-permute-start(f32[2,2,32,128]{3,2,1,0:T(8,128)S(1)} %get-tuple-element.64), channel_id=1, source_target_pairs={{4,0},{8,4},{12,8},{16,12},{20,16},{24,20},{28,24},{5,1},{9,5},{13... | collective-permute-start | bytes 196616 | tf_op jit(solution)/shard_map/ppermute | solution.py:368
  12.6 7.6 %collective-permute-start.2 = (f32[2,6,2,32,128]{4,3,2,1,0:T(8,128)S(1)}, f32[2,6,2,32,128]{4,3,2,1,0:T(8,128)S(1)}, u32[]{:S(2)}, u32[]{:S(2)}) collective-permute-start(f32[2,6,2,32,128]{4,3,2,1,0:T(8,128)S(1)} %get-tuple-element.69.own.refs_0_), channel_id=1, source_target_pairs={{0,1},{1,0},{2,3},{3,2},{4,5},{5,4},{6,7},{7,6},{8,9},{9,8},{10,11... | collective-permute-start | bytes 1179656 | tf_op jit(solution)/shard_map/ppermute | solution.py:352
  12.7 0.7 collective-permute-start.3
  13.4 9.8 %collective-permute-start.4 = (f32[2,6,32,128]{3,2,1,0:T(8,128)S(1)}, f32[2,6,32,128]{3,2,1,0:T(8,128)S(1)}, u32[]{:S(2)}, u32[]{:S(2)}) collective-permute-start(f32[2,6,32,128]{3,2,1,0:T(8,128)S(1)} %collective-permute-done.3.outer.refs_2_), channel_id=1, source_target_pairs={{0,1},{1,0},{2,3},{3,2},{4,5},{5,4},{6,7},{7,6},{8,9},{9,8},{10,11... | collective-permute-start | bytes 589832 | tf_op jit(solution)/shard_map/ppermute | solution.py:352
  23.1 1.4 %collective-permute-start.5 = (f32[4,2,32,128]{3,2,1,0:T(8,128)S(1)}, f32[4,2,32,128]{3,2,1,0:T(8,128)S(1)}, u32[]{:S(2)}, u32[]{:S(2)}) collective-permute-start(f32[4,2,32,128]{3,2,1,0:T(8,128)S(1)} %get-tuple-element.75), channel_id=1, source_target_pairs={{0,1},{1,0},{2,3},{3,2},{4,5},{5,4},{6,7},{7,6},{8,9},{9,8},{10,11... | collective-permute-start | bytes 393224 | tf_op jit(solution)/shard_map/ppermute | solution.py:352
  26.4 12.6 %collective-permute-start.6 = (f32[7,128,128]{2,1,0:T(8,128)S(1)}, f32[7,128,128]{2,1,0:T(8,128)S(1)}, u32[]{:S(2)}, u32[]{:S(2)}) collective-permute-start(f32[7,128,128]{2,1,0:T(8,128)S(1)} %get-tuple-element.84), channel_id=1, source_target_pairs={{0,2},{1,3},{2,0},{3,1},{4,6},{5,7},{6,4},{7,5},{8,10},{9,11},{10,... | collective-permute-start | bytes 1376264 | tf_op jit(solution)/shard_map/ppermute | solution.py:352
  27.6 13.2 %collective-permute-start.7 = (f32[7,128,128]{2,1,0:T(8,128)S(1)}, f32[7,128,128]{2,1,0:T(8,128)S(1)}, u32[]{:S(2)}, u32[]{:S(2)}) collective-permute-start(f32[7,128,128]{2,1,0:T(8,128)S(1)} %get-tuple-element.85), channel_id=1, source_target_pairs={{0,4},{4,0},{8,12},{12,8},{16,20},{20,16},{24,28},{28,24},{1,5},{5... | collective-permute-start | bytes 1376264 | tf_op jit(solution)/shard_map/ppermute | solution.py:352
  41.0 7.1 %collective-permute-start.8 = (f32[448,128]{1,0:T(8,128)S(1)}, f32[448,128]{1,0:T(8,128)S(1)}, u32[]{:S(2)}, u32[]{:S(2)}) collective-permute-start(f32[448,128]{1,0:T(8,128)S(1)} %get-tuple-element.88), channel_id=1, source_target_pairs={{0,4},{4,0},{8,12},{12,8},{16,20},{20,16},{24,28},{28,24},{1,5},{5... | collective-permute-start | bytes 688136 | tf_op jit(solution)/shard_map/ppermute | solution.py:352
  42.8 6.5 %collective-permute-start.9 = (f32[448,128]{1,0:T(8,128)S(1)}, f32[448,128]{1,0:T(8,128)S(1)}, u32[]{:S(2)}, u32[]{:S(2)}) collective-permute-start(f32[448,128]{1,0:T(8,128)S(1)} %get-tuple-element.89), channel_id=1, source_target_pairs={{0,2},{1,3},{2,0},{3,1},{4,6},{5,7},{6,4},{7,5},{8,10},{9,11},{10,... | collective-permute-start | bytes 688136 | tf_op jit(solution)/shard_map/ppermute | solution.py:352
  49.3 5.3 %collective-permute-start.10 = (f32[2,112,128]{2,1,0:T(8,128)S(1)}, f32[2,112,128]{2,1,0:T(8,128)S(1)}, u32[]{:S(2)}, u32[]{:S(2)}) collective-permute-start(f32[2,112,128]{2,1,0:T(8,128)S(1)} %get-tuple-element.91), channel_id=1, source_target_pairs={{0,8},{4,12},{8,0},{12,4},{16,24},{20,28},{24,16},{28,20},{1,9},{5... | collective-permute-start | bytes 344072 | tf_op jit(solution)/shard_map/ppermute | solution.py:352
  50.9 9.9 %collective-permute-start.11 = (f32[2,112,128]{2,1,0:T(8,128)S(1)}, f32[2,112,128]{2,1,0:T(8,128)S(1)}, u32[]{:S(2)}, u32[]{:S(2)}) collective-permute-start(f32[2,112,128]{2,1,0:T(8,128)S(1)} %get-tuple-element.92), channel_id=1, source_target_pairs={{0,16},{4,20},{8,24},{12,28},{16,0},{20,4},{24,8},{28,12},{1,17},{... | collective-permute-start | bytes 344072 | tf_op jit(solution)/shard_map/ppermute | solution.py:352
  52.0 8.8 %collective-permute-start.12 = (f32[2,112,128]{2,1,0:T(8,128)S(1)}, f32[2,112,128]{2,1,0:T(8,128)S(1)}, u32[]{:S(2)}, u32[]{:S(2)}) collective-permute-start(f32[2,112,128]{2,1,0:T(8,128)S(1)} %get-tuple-element.93), channel_id=1, source_target_pairs={{0,24},{4,28},{8,16},{12,20},{16,8},{20,12},{24,0},{28,4},{1,25},{... | collective-permute-start | bytes 344072 | tf_op jit(solution)/shard_map/ppermute | solution.py:352
  60.9 45.3 %copy-start = (f32[4,2,32,128]{3,2,1,0:T(8,128)S(1)}, f32[4,2,32,128]{3,2,1,0:T(8,128)}, u32[]{:S(2)}) copy-start(f32[4,2,32,128]{3,2,1,0:T(8,128)} %clip.1) | copy-start | bytes 393220
  60.9 45.3 %copy-start.1 = (f32[4,2,32,128]{3,2,1,0:T(8,128)S(1)}, f32[4,2,32,128]{3,2,1,0:T(8,128)}, u32[]{:S(2)}) copy-start(f32[4,2,32,128]{3,2,1,0:T(8,128)} %cotangent.1) | copy-start | bytes 393220
  60.9 6.0 %collective-permute-start.13 = (f32[2,112,128]{2,1,0:T(8,128)S(1)}, f32[2,112,128]{2,1,0:T(8,128)S(1)}, u32[]{:S(2)}, u32[]{:S(2)}) collective-permute-start(f32[2,112,128]{2,1,0:T(8,128)S(1)} %shard_map.84.q0), channel_id=1, source_target_pairs={{0,8},{4,12},{8,0},{12,4},{16,24},{20,28},{24,16},{28,20},{1,9},{5... | collective-permute-start | bytes 344072 | tf_op jit(solution)/shard_map/ppermute | solution.py:352
  62.8 11.0 %collective-permute-start.14 = (f32[2,112,128]{2,1,0:T(8,128)S(1)}, f32[2,112,128]{2,1,0:T(8,128)S(1)}, u32[]{:S(2)}, u32[]{:S(2)}) collective-permute-start(f32[2,112,128]{2,1,0:T(8,128)S(1)} %shard_map.84.q0), channel_id=1, source_target_pairs={{0,16},{4,20},{8,24},{12,28},{16,0},{20,4},{24,8},{28,12},{1,17},{... | collective-permute-start | bytes 344072 | tf_op jit(solution)/shard_map/ppermute | solution.py:352
  63.8 9.9 %collective-permute-start.15 = (f32[2,112,128]{2,1,0:T(8,128)S(1)}, f32[2,112,128]{2,1,0:T(8,128)S(1)}, u32[]{:S(2)}, u32[]{:S(2)}) collective-permute-start(f32[2,112,128]{2,1,0:T(8,128)S(1)} %shard_map.84.q0), channel_id=1, source_target_pairs={{0,24},{4,28},{8,16},{12,20},{16,8},{20,12},{24,0},{28,4},{1,25},{... | collective-permute-start | bytes 344072 | tf_op jit(solution)/shard_map/ppermute | solution.py:352
  73.8 6.1 %collective-permute-start.16 = (f32[448,128]{1,0:T(8,128)S(1)}, f32[448,128]{1,0:T(8,128)S(1)}, u32[]{:S(2)}, u32[]{:S(2)}) collective-permute-start(f32[448,128]{1,0:T(8,128)S(1)} %get-tuple-element.94.own_a), channel_id=1, source_target_pairs={{0,4},{4,0},{8,12},{12,8},{16,20},{20,16},{24,28},{28,24},{1,5},{5... | collective-permute-start | bytes 688136 | tf_op jit(solution)/shard_map/ppermute | solution.py:352
  74.7 6.0 %collective-permute-start.17 = (f32[448,128]{1,0:T(8,128)S(1)}, f32[448,128]{1,0:T(8,128)S(1)}, u32[]{:S(2)}, u32[]{:S(2)}) collective-permute-start(f32[448,128]{1,0:T(8,128)S(1)} %get-tuple-element.95.own_b), channel_id=1, source_target_pairs={{0,2},{1,3},{2,0},{3,1},{4,6},{5,7},{6,4},{7,5},{8,10},{9,11},{10,... | collective-permute-start | bytes 688136 | tf_op jit(solution)/shard_map/ppermute | solution.py:352
  80.8 20.9 %collective-permute-start.22 = (f32[896,128]{1,0:T(8,128)S(1)}, f32[896,128]{1,0:T(8,128)S(1)}, u32[]{:S(2)}, u32[]{:S(2)}) collective-permute-start(f32[896,128]{1,0:T(8,128)S(1)} %get-tuple-element.96), channel_id=1, source_target_pairs={{0,1},{1,0},{2,3},{3,2},{4,5},{5,4},{6,7},{7,6},{8,9},{9,8},{10,11... | collective-permute-start | bytes 1376264 | tf_op jit(solution)/shard_map/ppermute | solution.py:352
  80.9 23.8 %collective-permute-start.23 = (f32[896,128]{1,0:T(8,128)S(1)}, f32[896,128]{1,0:T(8,128)S(1)}, u32[]{:S(2)}, u32[]{:S(2)}) collective-permute-start(f32[896,128]{1,0:T(8,128)S(1)} %get-tuple-element.97), channel_id=1, source_target_pairs={{0,1},{1,0},{2,3},{3,2},{4,5},{5,4},{6,7},{7,6},{8,9},{9,8},{10,11... | collective-permute-start | bytes 1376264 | tf_op jit(solution)/shard_map/ppermute | solution.py:352
  81.4 28.5 %collective-permute-start.18 = (f32[896,128]{1,0:T(8,128)S(1)}, f32[896,128]{1,0:T(8,128)S(1)}, u32[]{:S(2)}, u32[]{:S(2)}) collective-permute-start(f32[896,128]{1,0:T(8,128)S(1)} %get-tuple-element.96), channel_id=1, source_target_pairs={{0,2},{1,3},{2,0},{3,1},{4,6},{5,7},{6,4},{7,5},{8,10},{9,11},{10,... | collective-permute-start | bytes 1376264 | tf_op jit(solution)/shard_map/ppermute | solution.py:352
  81.6 28.2 %collective-permute-start.19 = (f32[896,128]{1,0:T(8,128)S(1)}, f32[896,128]{1,0:T(8,128)S(1)}, u32[]{:S(2)}, u32[]{:S(2)}) collective-permute-start(f32[896,128]{1,0:T(8,128)S(1)} %get-tuple-element.97), channel_id=1, source_target_pairs={{0,4},{4,0},{8,12},{12,8},{16,20},{20,16},{24,28},{28,24},{1,5},{5... | collective-permute-start | bytes 1376264 | tf_op jit(solution)/shard_map/ppermute | solution.py:352
  83.1 11.1 %collective-permute-start.20 = (f32[2,2,32,128]{3,2,1,0:T(8,128)S(1)}, f32[2,2,32,128]{3,2,1,0:T(8,128)S(1)}, u32[]{:S(2)}, u32[]{:S(2)}) collective-permute-start(f32[2,2,32,128]{3,2,1,0:T(8,128)S(1)} %get-tuple-element.98), channel_id=1, source_target_pairs={{0,4},{4,8},{8,12},{12,16},{16,20},{20,24},{24,28},{1,5},{5,9},{9,... | collective-permute-start | bytes 196616 | tf_op jit(solution)/shard_map/ppermute | solution.py:408
  94.2 6.6 %collective-permute-start.21 = (f32[2,2,32,128]{3,2,1,0:T(8,128)S(1)}, f32[2,2,32,128]{3,2,1,0:T(8,128)S(1)}, u32[]{:S(2)}, u32[]{:S(2)}) collective-permute-start(f32[2,2,32,128]{3,2,1,0:T(8,128)S(1)} %get-tuple-element.99), channel_id=1, source_target_pairs={{4,0},{8,4},{12,8},{16,12},{20,16},{24,20},{28,24},{5,1},{9,5},{13... | collective-permute-start | bytes 196616 | tf_op jit(solution)/shard_map/ppermute | solution.py:409
  100.9 5.3 %collective-permute-start.24 = (f32[2,6,32,128]{3,2,1,0:T(8,128)S(1)}, f32[2,6,32,128]{3,2,1,0:T(8,128)S(1)}, u32[]{:S(2)}, u32[]{:S(2)}) collective-permute-start(f32[2,6,32,128]{3,2,1,0:T(8,128)S(1)} %get-tuple-element.102), channel_id=1, source_target_pairs={{1,2},{2,1},{5,6},{6,5},{9,10},{10,9},{13,14},{14,13},{17,18},{18,... | collective-permute-start | bytes 589832 | tf_op jit(solution)/shard_map/ppermute | solution.py:420
  101.8 4.4 %collective-permute-start.25 = (f32[2,6,32,128]{3,2,1,0:T(8,128)S(1)}, f32[2,6,32,128]{3,2,1,0:T(8,128)S(1)}, u32[]{:S(2)}, u32[]{:S(2)}) collective-permute-start(f32[2,6,32,128]{3,2,1,0:T(8,128)S(1)} %get-tuple-element.103), channel_id=1, source_target_pairs={{0,1},{1,0},{2,3},{3,2},{4,5},{5,4},{6,7},{7,6},{8,9},{9,8},{10,11... | collective-permute-start | bytes 589832 | tf_op jit(solution)/shard_map/ppermute | solution.py:352
  109.9 3.0 %collective-permute-start.26 = (f32[896,128]{1,0:T(8,128)S(1)}, f32[896,128]{1,0:T(8,128)S(1)}, u32[]{:S(2)}, u32[]{:S(2)}) collective-permute-start(f32[896,128]{1,0:T(8,128)S(1)} %collective-permute-done.18), channel_id=1, source_target_pairs={{0,1},{1,0},{2,3},{3,2},{4,5},{5,4},{6,7},{7,6},{8,9},{9,8},{10,11... | collective-permute-start | bytes 1376264 | tf_op jit(solution)/shard_map/ppermute | solution.py:352
  111.4 2.1 %collective-permute-start.27 = (f32[896,128]{1,0:T(8,128)S(1)}, f32[896,128]{1,0:T(8,128)S(1)}, u32[]{:S(2)}, u32[]{:S(2)}) collective-permute-start(f32[896,128]{1,0:T(8,128)S(1)} %collective-permute-done.19), channel_id=1, source_target_pairs={{0,1},{1,0},{2,3},{3,2},{4,5},{5,4},{6,7},{7,6},{8,9},{9,8},{10,11... | collective-permute-start | bytes 1376264 | tf_op jit(solution)/shard_map/ppermute | solution.py:352
where the time goes:
time: 117 us; the launch traced here: 115 us
  waiting for transfers between devices  53.7 us (46%)
  starting transfers between devices  41.4 us (35%)
  Pallas kernels  19.1 us (16%)
    ppermute x22, waiting for transfers between devices, swapped(): lax.ppermute(value, axis, [(i, i ^ bits) for i in range(lax.axis_size(axi...  37.1 us
    ppermute x22, starting transfers between devices, swapped(): lax.ppermute(value, axis, [(i, i ^ bits) for i in range(lax.axis_size(axi...  29.9 us
    pallas_call x16, Pallas kernels, kernel(): pl.pallas_call(body, out_shape=list(outs), in_specs=[pl.BlockSpec(memory_...  19.1 us
    ppermute x2, waiting for transfers between devices, per_device(): before = lax.ppermute(tail, 'tm', later)  8.66 us
    ppermute x2, waiting for transfers between devices, per_device(): after = lax.ppermute(head, 'tm', earlier)  7.85 us
    ppermute x2, starting transfers between devices, per_device(): before = lax.ppermute(tail, 'tm', later)  7.35 us
    ppermute x2, starting transfers between devices, per_device(): after = lax.ppermute(head, 'tm', earlier)  2.57 us
  transfers between devices with their start and end apart: 28, of which 16 were waited for; matrix products, arithmetic and copies ran while one was open for 0% of the time, Pallas kernels for 13%

commit v1 on v0

--- a/solution.py
+++ b/solution.py
@@ -182,10 +182,30 @@
     grad_clip[...] = cotangent[...] + convolve(strip, w_one, shifted, columns).reshape(clip.shape)
 
 
-def grads_body(sending, own, partner, outer, far, active, delta, arrived, first, second, field, wide, turned):
-    odd = lax.axis_index("rows") % 2
-    y_bit = (lax.axis_index("rows") // 2) % 2
-    x_bit = lax.axis_index("tm") % 2
+def bits_of():
+    row = lax.axis_index("rows")
+    return row % 2, (row // 2) % 2, lax.axis_index("tm") % 2
+
+
+def turn(value, turned):
+    ch = value.shape[-1]
+    high, low = halves(value.reshape(-1, ch).T)
+    turned[0:ch] = high
+    turned[ch : 2 * ch] = low
+
+
+def tap_sum(tap, turned, wide, frames, start, rows):
+    tap = jnp.minimum(tap, 26)
+    a, b, c = tap // 9, (tap // 3) % 3, tap % 3
+    ch = wide.shape[-1] // 2
+    piece = wide[c, pl.ds(a, frames), pl.ds(b + start, rows)].reshape(-1, 2 * ch)
+    product = jnp.dot(turned[...], piece, preferred_element_type=F32)
+    left = product[:, :ch] + product[:, ch:]
+    return left[:ch] + left[ch:]
+
+
+def near_body(own, partner, outer, far, active, delta, wide, first, second, field, turned):
+    odd, y_bit, x_bit = bits_of()
     tall, rows, span, ch = own.shape[1:]
     frames = active.shape[0]
     pick = 1 - odd
@@ -198,48 +218,32 @@
         high, low = halves(moved_column(flat, c - 1, span))
         wide[c, :, :, :, 0:ch] = high.reshape(field.shape)
         wide[c, :, :, :, ch : 2 * ch] = low.reshape(field.shape)
+    turn(jnp.where(odd == 0, active[...], delta[...]), turned)
+    for j in range(7):
+        first[j] = tap_sum((1 - y_bit) * 7 + j, turned, wide, frames, rows * odd, rows)
+        second[j] = tap_sum((3 - x_bit) * 7 + j, turned, wide, frames, rows * odd, rows)
+
+
+def give_body(wide, near_a, near_b, arrived, first, second, turned):
+    odd, y_bit, x_bit = bits_of()
+    frames, rows = arrived.shape[:2]
+    turn(arrived[...], turned)
+    for j in range(7):
+        first[j] = near_a[j] + tap_sum((1 - y_bit) * 7 + j, turned, wide, frames, rows * (1 - odd), rows)
+        second[j] = near_b[j] + tap_sum((3 - x_bit) * 7 + j, turned, wide, frames, rows * (1 - odd), rows)
+
+
+def keep_body(wide, active, delta, arrived, first, second, turned):
+    odd, y_bit, x_bit = bits_of()
+    frames, rows = arrived.shape[:2]
     mine = jnp.where(odd == 0, active[...], delta[...])
     other = arrived[...]
-    swap = odd == 1
-    upper = jnp.where(swap, other, mine)
-    lower = jnp.where(swap, mine, other)
-    cells = frames * 2 * rows * span
-    joined = jnp.concatenate([upper, lower], 1).reshape(cells, ch).T
-    high, low = halves(joined)
-    turned[0:ch] = high
-    turned[ch : 2 * ch] = low
-
-    def tap_of(group, j):
-        tap = jnp.minimum(group * 7 + j, 26)
-        a, b, c = tap // 9, (tap // 3) % 3, tap % 3
-        piece = wide[c, pl.ds(a, frames), pl.ds(b, 2 * rows)].reshape(cells, 2 * ch)
-        product = jnp.dot(turned[...], piece, preferred_element_type=F32)
-        left = product[:, :ch] + product[:, ch:]
-        return left[:ch] + left[ch:]
-
-    def step(j, carry):
-        first[j] = tap_of(y_bit ^ sending, j)
-        second[j] = tap_of(2 + (x_bit ^ sending), j)
-        return carry
-
-    lax.fori_loop(0, 7, step, 0, unroll=True)
-
-
-def grads(sending, own, partner, outer, far, active, delta, arrived):
-    frames, rows, span, ch = active.shape
-    out = shaped(7, ch, ch)
-    field = (frames + 2, 2 * rows + 2, span, ch)
-    return kernel(
-        lambda *refs: grads_body(sending, *refs),
-        [out, out],
-        (own, partner, outer, far, active, delta, arrived),
-        scratch=[
-            pltpu.VMEM(field, F32),
-            pltpu.VMEM((3, *field[:-1], 2 * ch), BF16),
-            pltpu.VMEM((2 * ch, frames * 2 * rows * span), BF16),
-        ],
-        flops=14 * 2 * (2 * ch) ** 2 * frames * 2 * rows * span,
-    )
+    upper = jnp.where(odd == 1, other, mine)
+    lower = jnp.where(odd == 1, mine, other)
+    turn(jnp.concatenate([upper, lower], 1), turned)
+    for j in range(7):
+        first[j] = tap_sum(y_bit * 7 + j, turned, wide, frames, 0, 2 * rows)
+        second[j] = tap_sum((2 + x_bit) * 7 + j, turned, wide, frames, 0, 2 * rows)
 
 
 def halve_body(keep_a, keep_b, got_a, got_b, stay_a, go_a, stay_b, go_b):
@@ -288,60 +292,53 @@
         out[pl.ds(pl.multiple_of((1 - bit) * half, 8), half)] = got[...]
 
 
-def finish_body(late, *refs):
-    mine, other = refs[0:2], refs[2:4]
+def finish_body(late, foreign, *refs):
+    sources = refs[:2]
     one, two, turned, sem = refs[-4:]
-    odd = lax.axis_index("rows") % 2
-    x_bit = lax.axis_index("tm") % 2
-    y_bit = (lax.axis_index("rows") // 2) % 2
+    odd, y_bit, x_bit = bits_of()
+    straight = odd == foreign
     groups = (y_bit ^ late, 2 + (x_bit ^ late))
     spots = [(k, j) for k in range(2) for j in range(7)]
 
-    def plain(k, j, source):
-        return pltpu.make_async_copy(source.at[j], two.at[26 - (groups[k] * 7 + j)], sem.at[0, k, j])
+    def plain(k, j):
+        return pltpu.make_async_copy(sources[k].at[j], two.at[26 - (groups[k] * 7 + j)], sem.at[k, j])
 
     def flipped(k, j):
-        return pltpu.make_async_copy(turned.at[k, j], one.at[groups[k] * 7 + j], sem.at[1, k, j])
-
-    for k, j in spots:
-        inside = groups[k] * 7 + j < 27
-
-        @pl.when(inside & (odd == 0))
-        def _():
-            plain(k, j, mine[k]).start()
-
-        @pl.when(inside & (odd == 1))
-        def _():
-            plain(k, j, other[k]).start()
-
-    for k in range(2):
-        for j in range(7):
-            turned[k, j] = jnp.where(odd == 0, other[k][j], mine[k][j]).T
-    for start in (True, False):
+        return pltpu.make_async_copy(turned.at[k, j], one.at[groups[k] * 7 + j], sem.at[k, j])
+
+    def each(make, act):
         for k, j in spots:
 
             @pl.when(groups[k] * 7 + j < 27)
             def _():
-                if start:
-                    flipped(k, j).start()
-                else:
-                    plain(k, j, mine[k]).wait()
-                    flipped(k, j).wait()
-
-
-def finish(late, mine, other, grads_so_far):
-    ch = mine[0].shape[-1]
+                act(make(k, j))
+
+    @pl.when(straight)
+    def _():
+        each(plain, lambda copy: copy.start())
+        each(plain, lambda copy: copy.wait())
+
+    @pl.when(jnp.logical_not(straight))
+    def _():
+        for k, j in spots:
+            turned[k, j] = sources[k][j].T
+        each(flipped, lambda copy: copy.start())
+        each(flipped, lambda copy: copy.wait())
+
+
+def finish(late, foreign, sources, grads_so_far):
+    ch = sources[0].shape[-1]
     grad = shaped(27, ch, ch)
-    args = [v.reshape(7, ch, ch) for v in (*mine, *other)] + list(grads_so_far)
-    return list(kernel(
-        lambda *refs: finish_body(late, *refs),
+    args = [v.reshape(7, ch, ch) for v in sources] + list(grads_so_far)
+    return kernel(
+        lambda *refs: finish_body(late, foreign, *refs),
         [grad, grad],
         args,
-        scratch=[pltpu.VMEM((2, 7, ch, ch), F32), pltpu.SemaphoreType.DMA((2, 2, 7))],
-        far_in=(4, 5),
+        scratch=[pltpu.VMEM((2, 7, ch, ch), F32), pltpu.SemaphoreType.DMA((2, 7))],
+        far_in=(2, 3),
         far_out=(0, 1),
-        alias={4: 0, 5: 1} if grads_so_far else None,
-    ))
+        alias={2: 0, 3: 1} if grads_so_far else None,
+    )
 
 
 def tied(*values):
@@ -385,11 +382,35 @@
     )
     arrived = swapped(crossing, "rows", 1)
 
-    shared = (own, partner, outer, far, active, delta, arrived)
-    give_a, give_b = grads(1, *shared)
+    piece = shaped(7, ch, ch)
+    tap_flops = 14 * 2 * (2 * ch) ** 2 * frames * rows * span
+    far, active = tied(far, active)
+    wide, near_a, near_b = kernel(
+        near_body,
+        [shaped(3, frames + 2, 2 * rows + 2, span, 2 * ch, kind=BF16), piece, piece],
+        (own, partner, outer, far, active, delta),
+        scratch=[
+            pltpu.VMEM((frames + 2, 2 * rows + 2, span, ch), F32),
+            pltpu.VMEM((2 * ch, frames * rows * span), BF16),
+        ],
+        flops=tap_flops,
+    )
+    give_a, give_b = kernel(
+        give_body,
+        [piece, piece],
+        (wide, near_a, near_b, arrived),
+        scratch=[pltpu.VMEM((2 * ch, frames * rows * span), BF16)],
+        flops=tap_flops,
+    )
     got_a = swapped(give_a, "rows", 2)
     got_b = swapped(give_b, "tm", 1)
-    keep_a, keep_b = grads(0, *shared)
+    keep_a, keep_b = kernel(
+        keep_body,
+        [piece, piece],
+        (wide, active, delta, arrived),
+        scratch=[pltpu.VMEM((2 * ch, 2 * frames * rows * span), BF16)],
+        flops=2 * tap_flops,
+    )
     keep_a, one, two = tied(keep_a, one, two)
     two_plain, one_turned = weights(two, one, ())
     keep_a, two_plain, one_turned = tied(keep_a, two_plain, one_turned)
@@ -426,7 +447,8 @@
     mine = kernel(join_halves_body, [full] * 2, (own_a, got_a, own_b, got_b))
     got = [swapped(mine[0], "rows", 2), swapped(mine[1], "tm", 1)]
     other = [swapped(v, "rows", 1) for v in mine]
-    half_done = finish(0, mine, other, ())
+    half_done = finish(0, 0, mine, ())
+    half_done = list(finish(0, 1, other, half_done))
     half_done[0], outer, inner = tied(half_done[0], outer, inner)
     block_out, grad_clip = kernel(
         outputs_body,
@@ -437,7 +459,8 @@
     )
     got[0], got[1], block_out, grad_clip = tied(*got, block_out, grad_clip)
     got_other = [swapped(v, "rows", 1) for v in got]
-    grad_one, grad_two = finish(1, got, got_other, half_done)
+    half_done = finish(1, 0, got, half_done)
+    grad_one, grad_two = finish(1, 1, got_other, half_done)
     shape = kernel_one.shape
     return block_out, grad_clip, grad_one.reshape(shape), grad_two.reshape(shape)
 

time: 117 us -> 115 us (0.983)
  waiting for transfers between devices: 53.7 us -> 48.3 us
  starting transfers between devices: 41.4 us -> 43.5 us
  Pallas kernels: 19.1 us -> 20.4 us
    ppermute x22, waiting for transfers between devices: 37.1 us -> 32.1 us  [swapped(): lax.ppermute(value, axis, [(i, i ^ bits) for i in range(lax.axis_size(axi...]
    ppermute x22, starting transfers between devices: 29.9 us -> 32 us  [swapped(): lax.ppermute(value, axis, [(i, i ^ bits) for i in range(lax.axis_size(axi...]
    pallas_call x16 -> x19, Pallas kernels: 19.1 us -> 20.4 us  [kernel(): pl.pallas_call(body, out_shape=list(outs), in_specs=[pl.BlockSpec(memory_...]
  transfers between devices with their start and end apart: 28 -> 28, of which waited for: 16 -> 15; matrix products, arithmetic and copies ran while one was open for 0% -> 0% of each run, Pallas kernels for 13% -> 15%
where the time goes in v1:
time: 115 us; the launch traced here: 113 us
  waiting for transfers between devices  48.3 us (42%)
  starting transfers between devices  43.5 us (38%)
  Pallas kernels  20.4 us (18%)
    ppermute x22, waiting for transfers between devices, swapped(): lax.ppermute(value, axis, [(i, i ^ bits) for i in range(lax.axis_size(axi...  32.1 us
    ppermute x22, starting transfers between devices, swapped(): lax.ppermute(value, axis, [(i, i ^ bits) for i in range(lax.axis_size(axi...  32 us
    pallas_call x19, Pallas kernels, kernel(): pl.pallas_call(body, out_shape=list(outs), in_specs=[pl.BlockSpec(memory_...  20.4 us
    ppermute x2, waiting for transfers between devices, per_device(): before = lax.ppermute(tail, 'tm', later)  8.4 us
    ppermute x2, waiting for transfers between devices, per_device(): after = lax.ppermute(head, 'tm', earlier)  7.85 us
    ppermute x2, starting transfers between devices, per_device(): before = lax.ppermute(tail, 'tm', later)  7.62 us
    ppermute x2, starting transfers between devices, per_device(): after = lax.ppermute(head, 'tm', earlier)  2.57 us
  transfers between devices with their start and end apart: 28, of which 15 were waited for; matrix products, arithmetic and copies ran while one was open for 0% of the time, Pallas kernels for 15%

profile of v1, /device:TPU:0, one launch (start us, length us, event | category | flops | bytes accessed | tf_op | source)
XLA Modules:
  0.0 113.3 jit_solution(10370504043487182702)
XLA Ops:
  1.5 4.9 %collective-permute-start = (f32[2,2,32,128]{3,2,1,0:T(8,128)S(1)}, f32[2,2,32,128]{3,2,1,0:T(8,128)S(1)}, u32[]{:S(2)}, u32[]{:S(2)}) collective-permute-start(f32[2,2,32,128]{3,2,1,0:T(8,128)S(1)} %get-tuple-element.72), channel_id=1, source_target_pairs={{0,4},{4,8},{8,12},{12,16},{16,20},{20,24},{24,28},{1,5},{5,9},{9,... | collective-permute-start | bytes 196616 | tf_op jit(solution)/shard_map/ppermute | solution.py:364
  6.4 1.3 %collective-permute-start.1 = (f32[2,2,32,128]{3,2,1,0:T(8,128)S(1)}, f32[2,2,32,128]{3,2,1,0:T(8,128)S(1)}, u32[]{:S(2)}, u32[]{:S(2)}) collective-permute-start(f32[2,2,32,128]{3,2,1,0:T(8,128)S(1)} %get-tuple-element.73), channel_id=1, source_target_pairs={{4,0},{8,4},{12,8},{16,12},{20,16},{24,20},{28,24},{5,1},{9,5},{13... | collective-permute-start | bytes 196616 | tf_op jit(solution)/shard_map/ppermute | solution.py:365
  7.7 2.3 %shard_map.75 = (bf16[27,128,256]{2,1,0:T(8,128)(2,1)S(1)}, bf16[27,128,256]{2,1,0:T(8,128)(2,1)S(1)}, f32[4,2,32,128]{3,2,1,0:T(8,128)S(1)}, f32[4,2,32,128]{3,2,1,0:T(8,128)S(1)}) custom-call(f32[27,128,128]{2,1,0:T(8,128)} %bitcast.30, f32[27,128,128]{2,1,0:T(8,128)} %bitcast.32, f32[4,2,32,128]{3,2,1,0:T(8,128)} %clip.1, f32[4,2,32,128]{3,2,1,0:T(8,128)} %cotangent.1), custom_call_target="tpu_custom_call" | custom-call | bytes 7602176 | tf_op jit(solution)/shard_map/pallas_call | solution.py:21
  10.0 2.5 %collective-permute-done.1.after = f32[2,2,32,128]{3,2,1,0:T(8,128)S(1)} collective-permute-done((f32[2,2,32,128]{3,2,1,0:T(8,128)S(1)}, f32[2,2,32,128]{3,2,1,0:T(8,128)S(1)}, u32[]{:S(2)}, u32[]{:S(2)}) %collective-permute-start.1) | collective-permute-done | bytes 65568 | tf_op jit(solution)/shard_map/ppermute | solution.py:365
  13.4 6.8 %collective-permute-start.4 = (f32[2,6,32,128]{3,2,1,0:T(8,128)S(1)}, f32[2,6,32,128]{3,2,1,0:T(8,128)S(1)}, u32[]{:S(2)}, u32[]{:S(2)}) collective-permute-start(f32[2,6,32,128]{3,2,1,0:T(8,128)S(1)} %collective-permute-done.3.outer), channel_id=1, source_target_pairs={{0,1},{1,0},{2,3},{3,2},{4,5},{5,4},{6,7},{7,6},{8,9},{9,8},{10,11... | collective-permute-start | bytes 589832 | tf_op jit(solution)/shard_map/ppermute | solution.py:349
  20.2 3.0 %shard_map.78 = (f32[4,2,32,128]{3,2,1,0:T(8,128)S(1)}, f32[4,2,32,128]{3,2,1,0:T(8,128)S(1)}, f32[2,2,32,128]{3,2,1,0:T(8,128)S(1)}, f32[2,2,32,128]{3,2,1,0:T(8,128)S(1)}, f32[4,2,32,128]{3,2,1,0:T(8,128)S(1)}) custom-call(f32[2,6,2,32,128]{4,3,2,1,0:T(8,128)S(1)} %get-tuple-element.78.own, f32[2,6,2,32,128]{4,3,2,1,0:T(8,128)S(1)} %collective-permute-done.2.partner, ...), custom_call_target="tpu_custom_call" | custom-call | flops 1358954496 | bytes 5046272 | tf_op jit(solution)/shard_map/pallas_call | solution.py:21
  23.2 1.3 %shard_map.79 = (bf16[3,6,6,32,256]{4,3,2,1,0:T(8,128)(2,1)S(1)}, f32[7,128,128]{2,1,0:T(8,128)S(1)}, f32[7,128,128]{2,1,0:T(8,128)S(1)}) custom-call(f32[2,6,2,32,128]{4,3,2,1,0:T(8,128)S(1)} %get-tuple-element.78.own, f32[2,6,2,32,128]{4,3,2,1,0:T(8,128)S(1)} %collective-permute-done.2.partner, f32[2,6,32,128]{3,2,1,0:T(8,128)S(1)} %collective-permute-done.3.outer, ...), custom_call_target="tpu_custom_call" | custom-call | flops 469762048 | bytes 4128768 | tf_op jit(solution)/shard_map/pallas_call | solution.py:21
  25.3 1.6 %collective-permute-start.6 = (f32[7,128,128]{2,1,0:T(8,128)S(1)}, f32[7,128,128]{2,1,0:T(8,128)S(1)}, u32[]{:S(2)}, u32[]{:S(2)}) collective-permute-start(f32[7,128,128]{2,1,0:T(8,128)S(1)} %get-tuple-element.98), channel_id=1, source_target_pairs={{0,2},{1,3},{2,0},{3,1},{4,6},{5,7},{6,4},{7,5},{8,10},{9,11},{10,... | collective-permute-start | bytes 1376264 | tf_op jit(solution)/shard_map/ppermute | solution.py:349
  26.9 2.4 %collective-permute-start.7 = (f32[7,128,128]{2,1,0:T(8,128)S(1)}, f32[7,128,128]{2,1,0:T(8,128)S(1)}, u32[]{:S(2)}, u32[]{:S(2)}) collective-permute-start(f32[7,128,128]{2,1,0:T(8,128)S(1)} %get-tuple-element.99), channel_id=1, source_target_pairs={{0,4},{4,0},{8,12},{12,8},{16,20},{20,16},{24,28},{28,24},{1,5},{5... | collective-permute-start | bytes 1376264 | tf_op jit(solution)/shard_map/ppermute | solution.py:349
  30.5 2.3 %shard_map.81 = (bf16[27,128,256]{2,1,0:T(8,128)(2,1)S(1)}, bf16[27,128,256]{2,1,0:T(8,128)(2,1)S(1)}) custom-call(f32[27,128,128]{2,1,0:T(8,128)} %bitcast.33, f32[27,128,128]{2,1,0:T(8,128)} %bitcast.31), custom_call_target="tpu_custom_call" | custom-call | bytes 7077888 | tf_op jit(solution)/shard_map/pallas_call | solution.py:21
  32.8 5.4 %collective-permute-done.6 = f32[7,128,128]{2,1,0:T(8,128)S(1)} collective-permute-done((f32[7,128,128]{2,1,0:T(8,128)S(1)}, f32[7,128,128]{2,1,0:T(8,128)S(1)}, u32[]{:S(2)}, u32[]{:S(2)}) %collective-permute-start.6) | collective-permute-done | bytes 458784 | tf_op jit(solution)/shard_map/ppermute | solution.py:349
  38.3 1.5 %collective-permute-done.7 = f32[7,128,128]{2,1,0:T(8,128)S(1)} collective-permute-done((f32[7,128,128]{2,1,0:T(8,128)S(1)}, f32[7,128,128]{2,1,0:T(8,128)S(1)}, u32[]{:S(2)}, u32[]{:S(2)}) %collective-permute-start.7) | collective-permute-done | bytes 458784 | tf_op jit(solution)/shard_map/ppermute | solution.py:349
  39.8 1.8 %collective-permute-start.8 = (f32[448,128]{1,0:T(8,128)S(1)}, f32[448,128]{1,0:T(8,128)S(1)}, u32[]{:S(2)}, u32[]{:S(2)}) collective-permute-start(f32[448,128]{1,0:T(8,128)S(1)} %get-tuple-element.102), channel_id=1, source_target_pairs={{0,4},{4,0},{8,12},{12,8},{16,20},{20,16},{24,28},{28,24},{1,5},{5... | collective-permute-start | bytes 688136 | tf_op jit(solution)/shard_map/ppermute | solution.py:349
  42.6 4.0 %collective-permute-done.8.got_a = f32[448,128]{1,0:T(8,128)S(1)} collective-permute-done((f32[448,128]{1,0:T(8,128)S(1)}, f32[448,128]{1,0:T(8,128)S(1)}, u32[]{:S(2)}, u32[]{:S(2)}) %collective-permute-start.8) | collective-permute-done | bytes 229408 | tf_op jit(solution)/shard_map/ppermute | solution.py:349
  47.8 1.6 %collective-permute-start.10 = (f32[2,112,128]{2,1,0:T(8,128)S(1)}, f32[2,112,128]{2,1,0:T(8,128)S(1)}, u32[]{:S(2)}, u32[]{:S(2)}) collective-permute-start(f32[2,112,128]{2,1,0:T(8,128)S(1)} %get-tuple-element.105), channel_id=1, source_target_pairs={{0,8},{4,12},{8,0},{12,4},{16,24},{20,28},{24,16},{28,20},{1,9},{5... | collective-permute-start | bytes 344072 | tf_op jit(solution)/shard_map/ppermute | solution.py:349
  50.6 1.7 %collective-permute-start.12 = (f32[2,112,128]{2,1,0:T(8,128)S(1)}, f32[2,112,128]{2,1,0:T(8,128)S(1)}, u32[]{:S(2)}, u32[]{:S(2)}) collective-permute-start(f32[2,112,128]{2,1,0:T(8,128)S(1)} %get-tuple-element.107), channel_id=1, source_target_pairs={{0,24},{4,28},{8,16},{12,20},{16,8},{20,12},{24,0},{28,4},{1,25},{... | collective-permute-start | bytes 344072 | tf_op jit(solution)/shard_map/ppermute | solution.py:349
  52.8 6.2 %collective-permute-done.11.refs_2_ = f32[2,112,128]{2,1,0:T(8,128)S(1)} collective-permute-done((f32[2,112,128]{2,1,0:T(8,128)S(1)}, f32[2,112,128]{2,1,0:T(8,128)S(1)}, u32[]{:S(2)}, u32[]{:S(2)}) %collective-permute-start.11) | collective-permute-done | bytes 114720 | tf_op jit(solution)/shard_map/ppermute | solution.py:349
  59.1 1.9 %collective-permute-start.13 = (f32[2,112,128]{2,1,0:T(8,128)S(1)}, f32[2,112,128]{2,1,0:T(8,128)S(1)}, u32[]{:S(2)}, u32[]{:S(2)}) collective-permute-start(f32[2,112,128]{2,1,0:T(8,128)S(1)} %shard_map.85.q0), channel_id=1, source_target_pairs={{0,8},{4,12},{8,0},{12,4},{16,24},{20,28},{24,16},{28,20},{1,9},{5... | collective-permute-start | bytes 344072 | tf_op jit(solution)/shard_map/ppermute | solution.py:349
  62.0 1.5 %collective-permute-start.15 = (f32[2,112,128]{2,1,0:T(8,128)S(1)}, f32[2,112,128]{2,1,0:T(8,128)S(1)}, u32[]{:S(2)}, u32[]{:S(2)}) collective-permute-start(f32[2,112,128]{2,1,0:T(8,128)S(1)} %shard_map.85.q0), channel_id=1, source_target_pairs={{0,24},{4,28},{8,16},{12,20},{16,8},{20,12},{24,0},{28,4},{1,25},{... | collective-permute-start | bytes 344072 | tf_op jit(solution)/shard_map/ppermute | solution.py:349
  63.5 1.6 %collective-permute-done.13.q1 = f32[2,112,128]{2,1,0:T(8,128)S(1)} collective-permute-done((f32[2,112,128]{2,1,0:T(8,128)S(1)}, f32[2,112,128]{2,1,0:T(8,128)S(1)}, u32[]{:S(2)}, u32[]{:S(2)}) %collective-permute-start.13) | collective-permute-done | bytes 114720 | tf_op jit(solution)/shard_map/ppermute | solution.py:349
  65.1 6.5 %collective-permute-done.14.q2 = f32[2,112,128]{2,1,0:T(8,128)S(1)} collective-permute-done((f32[2,112,128]{2,1,0:T(8,128)S(1)}, f32[2,112,128]{2,1,0:T(8,128)S(1)}, u32[]{:S(2)}, u32[]{:S(2)}) %collective-permute-start.14) | collective-permute-done | bytes 114720 | tf_op jit(solution)/shard_map/ppermute | solution.py:349
  72.8 1.9 %collective-permute-start.17 = (f32[448,128]{1,0:T(8,128)S(1)}, f32[448,128]{1,0:T(8,128)S(1)}, u32[]{:S(2)}, u32[]{:S(2)}) collective-permute-start(f32[448,128]{1,0:T(8,128)S(1)} %get-tuple-element.109.own_b), channel_id=1, source_target_pairs={{0,2},{1,3},{2,0},{3,1},{4,6},{5,7},{6,4},{7,5},{8,10},{9,11},{10,... | collective-permute-start | bytes 688136 | tf_op jit(solution)/shard_map/ppermute | solution.py:349
  74.8 3.0 %collective-permute-done.16.got_a = f32[448,128]{1,0:T(8,128)S(1)} collective-permute-done((f32[448,128]{1,0:T(8,128)S(1)}, f32[448,128]{1,0:T(8,128)S(1)}, u32[]{:S(2)}, u32[]{:S(2)}) %collective-permute-start.16) | collective-permute-done | bytes 229408 | tf_op jit(solution)/shard_map/ppermute | solution.py:349
  79.5 1.9 %collective-permute-start.18 = (f32[896,128]{1,0:T(8,128)S(1)}, f32[896,128]{1,0:T(8,128)S(1)}, u32[]{:S(2)}, u32[]{:S(2)}) collective-permute-start(f32[896,128]{1,0:T(8,128)S(1)} %get-tuple-element.110), channel_id=1, source_target_pairs={{0,2},{1,3},{2,0},{3,1},{4,6},{5,7},{6,4},{7,5},{8,10},{9,11},{10,... | collective-permute-start | bytes 1376264 | tf_op jit(solution)/shard_map/ppermute | solution.py:349
  82.6 2.7 %collective-permute-start.20 = (f32[2,2,32,128]{3,2,1,0:T(8,128)S(1)}, f32[2,2,32,128]{3,2,1,0:T(8,128)S(1)}, u32[]{:S(2)}, u32[]{:S(2)}) collective-permute-start(f32[2,2,32,128]{3,2,1,0:T(8,128)S(1)} %get-tuple-element.112), channel_id=1, source_target_pairs={{0,4},{4,8},{8,12},{12,16},{16,20},{20,24},{24,28},{1,5},{5,9},{9,... | collective-permute-start | bytes 196616 | tf_op jit(solution)/shard_map/ppermute | solution.py:429
  85.4 8.4 %collective-permute-done.20.before = f32[2,2,32,128]{3,2,1,0:T(8,128)S(1)} collective-permute-done((f32[2,2,32,128]{3,2,1,0:T(8,128)S(1)}, f32[2,2,32,128]{3,2,1,0:T(8,128)S(1)}, u32[]{:S(2)}, u32[]{:S(2)}) %collective-permute-start.20) | collective-permute-done | bytes 65568 | tf_op jit(solution)/shard_map/ppermute | solution.py:429
  93.8 1.3 %collective-permute-start.21 = (f32[2,2,32,128]{3,2,1,0:T(8,128)S(1)}, f32[2,2,32,128]{3,2,1,0:T(8,128)S(1)}, u32[]{:S(2)}, u32[]{:S(2)}) collective-permute-start(f32[2,2,32,128]{3,2,1,0:T(8,128)S(1)} %get-tuple-element.113), channel_id=1, source_target_pairs={{4,0},{8,4},{12,8},{16,12},{20,16},{24,20},{28,24},{5,1},{9,5},{13... | collective-permute-start | bytes 196616 | tf_op jit(solution)/shard_map/ppermute | solution.py:430
  95.1 5.3 %collective-permute-done.21.after = f32[2,2,32,128]{3,2,1,0:T(8,128)S(1)} collective-permute-done((f32[2,2,32,128]{3,2,1,0:T(8,128)S(1)}, f32[2,2,32,128]{3,2,1,0:T(8,128)S(1)}, u32[]{:S(2)}, u32[]{:S(2)}) %collective-permute-start.21) | collective-permute-done | bytes 65568 | tf_op jit(solution)/shard_map/ppermute | solution.py:430
  101.1 1.7 %collective-permute-start.25 = (f32[2,6,32,128]{3,2,1,0:T(8,128)S(1)}, f32[2,6,32,128]{3,2,1,0:T(8,128)S(1)}, u32[]{:S(2)}, u32[]{:S(2)}) collective-permute-start(f32[2,6,32,128]{3,2,1,0:T(8,128)S(1)} %get-tuple-element.119), channel_id=1, source_target_pairs={{0,1},{1,0},{2,3},{3,2},{4,5},{5,4},{6,7},{7,6},{8,9},{9,8},{10,11... | collective-permute-start | bytes 589832 | tf_op jit(solution)/shard_map/ppermute | solution.py:349
  103.9 1.4 %shard_map.90 = (f32[27,128,128]{2,1,0:T(8,128)}, f32[27,128,128]{2,1,0:T(8,128)}) custom-call(f32[7,128,128]{2,1,0:T(8,128)S(1)} %bitcast.18, f32[7,128,128]{2,1,0:T(8,128)S(1)} %bitcast.19, f32[27,128,128]{2,1,0:T(8,128)} %get-tuple-element.115.refs_2_, f32[27,128,128]{2,1,0:T(8,128)} %get-tuple-element.116.refs_3_), custom_call_target="tpu_custom_call", output_to_operand_aliasing={{0}: (2, {}), {1}: (3, {})} | custom-call | bytes 7995392 | tf_op jit(solution)/shard_map/pallas_call | solution.py:21
  105.3 3.6 %shard_map.91 = (f32[4,2,32,128]{3,2,1,0:T(8,128)}, f32[4,2,32,128]{3,2,1,0:T(8,128)}) custom-call(f32[2,6,2,32,128]{4,3,2,1,0:T(8,128)S(1)} %get-tuple-element.114.ext, f32[2,6,32,128]{3,2,1,0:T(8,128)S(1)} %collective-permute-done.24.outer, f32[2,6,32,128]{3,2,1,0:T(8,128)S(1)} %collective-permute-done.25.inner, ...), custom_call_target="tpu_custom_call" | custom-call | flops 1358954496 | bytes 4849664 | tf_op jit(solution)/shard_map/pallas_call | solution.py:21
  111.8 1.3 %shard_map.93 = (f32[27,128,128]{2,1,0:T(8,128)}, f32[27,128,128]{2,1,0:T(8,128)}) custom-call(f32[7,128,128]{2,1,0:T(8,128)S(1)} %bitcast.20, f32[7,128,128]{2,1,0:T(8,128)S(1)} %bitcast.21, f32[27,128,128]{2,1,0:T(8,128)} %get-tuple-element.132.refs_2_, f32[27,128,128]{2,1,0:T(8,128)} %get-tuple-element.133.refs_3_), custom_call_target="tpu_custom_call", output_to_operand_aliasing={{0}: (2, {}), {1}: (3, {})} | custom-call | bytes 7995392 | tf_op jit(solution)/shard_map/pallas_call | solution.py:21
  (47 shorter events, 17.5 us)
Async XLA Ops:
  1.5 8.5 %collective-permute-start = (f32[2,2,32,128]{3,2,1,0:T(8,128)S(1)}, f32[2,2,32,128]{3,2,1,0:T(8,128)S(1)}, u32[]{:S(2)}, u32[]{:S(2)}) collective-permute-start(f32[2,2,32,128]{3,2,1,0:T(8,128)S(1)} %get-tuple-element.72), channel_id=1, source_target_pairs={{0,4},{4,8},{8,12},{12,16},{16,20},{20,24},{24,28},{1,5},{5,9},{9,... | collective-permute-start | bytes 196616 | tf_op jit(solution)/shard_map/ppermute | solution.py:364
  6.4 6.2 %collective-permute-start.1 = (f32[2,2,32,128]{3,2,1,0:T(8,128)S(1)}, f32[2,2,32,128]{3,2,1,0:T(8,128)S(1)}, u32[]{:S(2)}, u32[]{:S(2)}) collective-permute-start(f32[2,2,32,128]{3,2,1,0:T(8,128)S(1)} %get-tuple-element.73), channel_id=1, source_target_pairs={{4,0},{8,4},{12,8},{16,12},{20,16},{24,20},{28,24},{5,1},{9,5},{13... | collective-permute-start | bytes 196616 | tf_op jit(solution)/shard_map/ppermute | solution.py:365
  12.6 7.6 %collective-permute-start.2 = (f32[2,6,2,32,128]{4,3,2,1,0:T(8,128)S(1)}, f32[2,6,2,32,128]{4,3,2,1,0:T(8,128)S(1)}, u32[]{:S(2)}, u32[]{:S(2)}) collective-permute-start(f32[2,6,2,32,128]{4,3,2,1,0:T(8,128)S(1)} %get-tuple-element.78.own), channel_id=1, source_target_pairs={{0,1},{1,0},{2,3},{3,2},{4,5},{5,4},{6,7},{7,6},{8,9},{9,8},{10,11... | collective-permute-start | bytes 1179656 | tf_op jit(solution)/shard_map/ppermute | solution.py:349
  12.7 0.7 collective-permute-start.3
  13.4 9.8 %collective-permute-start.4 = (f32[2,6,32,128]{3,2,1,0:T(8,128)S(1)}, f32[2,6,32,128]{3,2,1,0:T(8,128)S(1)}, u32[]{:S(2)}, u32[]{:S(2)}) collective-permute-start(f32[2,6,32,128]{3,2,1,0:T(8,128)S(1)} %collective-permute-done.3.outer), channel_id=1, source_target_pairs={{0,1},{1,0},{2,3},{3,2},{4,5},{5,4},{6,7},{7,6},{8,9},{9,8},{10,11... | collective-permute-start | bytes 589832 | tf_op jit(solution)/shard_map/ppermute | solution.py:349
  23.1 1.4 %collective-permute-start.5 = (f32[4,2,32,128]{3,2,1,0:T(8,128)S(1)}, f32[4,2,32,128]{3,2,1,0:T(8,128)S(1)}, u32[]{:S(2)}, u32[]{:S(2)}) collective-permute-start(f32[4,2,32,128]{3,2,1,0:T(8,128)S(1)} %get-tuple-element.87), channel_id=1, source_target_pairs={{0,1},{1,0},{2,3},{3,2},{4,5},{5,4},{6,7},{7,6},{8,9},{9,8},{10,11... | collective-permute-start | bytes 393224 | tf_op jit(solution)/shard_map/ppermute | solution.py:349
  25.3 13.0 %collective-permute-start.6 = (f32[7,128,128]{2,1,0:T(8,128)S(1)}, f32[7,128,128]{2,1,0:T(8,128)S(1)}, u32[]{:S(2)}, u32[]{:S(2)}) collective-permute-start(f32[7,128,128]{2,1,0:T(8,128)S(1)} %get-tuple-element.98), channel_id=1, source_target_pairs={{0,2},{1,3},{2,0},{3,1},{4,6},{5,7},{6,4},{7,5},{8,10},{9,11},{10,... | collective-permute-start | bytes 1376264 | tf_op jit(solution)/shard_map/ppermute | solution.py:349
  26.9 12.9 %collective-permute-start.7 = (f32[7,128,128]{2,1,0:T(8,128)S(1)}, f32[7,128,128]{2,1,0:T(8,128)S(1)}, u32[]{:S(2)}, u32[]{:S(2)}) collective-permute-start(f32[7,128,128]{2,1,0:T(8,128)S(1)} %get-tuple-element.99), channel_id=1, source_target_pairs={{0,4},{4,0},{8,12},{12,8},{16,20},{20,16},{24,28},{28,24},{1,5},{5... | collective-permute-start | bytes 1376264 | tf_op jit(solution)/shard_map/ppermute | solution.py:349
  39.8 6.7 %collective-permute-start.8 = (f32[448,128]{1,0:T(8,128)S(1)}, f32[448,128]{1,0:T(8,128)S(1)}, u32[]{:S(2)}, u32[]{:S(2)}) collective-permute-start(f32[448,128]{1,0:T(8,128)S(1)} %get-tuple-element.102), channel_id=1, source_target_pairs={{0,4},{4,0},{8,12},{12,8},{16,20},{20,16},{24,28},{28,24},{1,5},{5... | collective-permute-start | bytes 688136 | tf_op jit(solution)/shard_map/ppermute | solution.py:349
  41.7 6.1 %collective-permute-start.9 = (f32[448,128]{1,0:T(8,128)S(1)}, f32[448,128]{1,0:T(8,128)S(1)}, u32[]{:S(2)}, u32[]{:S(2)}) collective-permute-start(f32[448,128]{1,0:T(8,128)S(1)} %get-tuple-element.103), channel_id=1, source_target_pairs={{0,2},{1,3},{2,0},{3,1},{4,6},{5,7},{6,4},{7,5},{8,10},{9,11},{10,... | collective-permute-start | bytes 688136 | tf_op jit(solution)/shard_map/ppermute | solution.py:349
  47.8 5.0 %collective-permute-start.10 = (f32[2,112,128]{2,1,0:T(8,128)S(1)}, f32[2,112,128]{2,1,0:T(8,128)S(1)}, u32[]{:S(2)}, u32[]{:S(2)}) collective-permute-start(f32[2,112,128]{2,1,0:T(8,128)S(1)} %get-tuple-element.105), channel_id=1, source_target_pairs={{0,8},{4,12},{8,0},{12,4},{16,24},{20,28},{24,16},{28,20},{1,9},{5... | collective-permute-start | bytes 344072 | tf_op jit(solution)/shard_map/ppermute | solution.py:349
  49.5 9.6 %collective-permute-start.11 = (f32[2,112,128]{2,1,0:T(8,128)S(1)}, f32[2,112,128]{2,1,0:T(8,128)S(1)}, u32[]{:S(2)}, u32[]{:S(2)}) collective-permute-start(f32[2,112,128]{2,1,0:T(8,128)S(1)} %get-tuple-element.106), channel_id=1, source_target_pairs={{0,16},{4,20},{8,24},{12,28},{16,0},{20,4},{24,8},{28,12},{1,17},{... | collective-permute-start | bytes 344072 | tf_op jit(solution)/shard_map/ppermute | solution.py:349
  50.6 8.5 %collective-permute-start.12 = (f32[2,112,128]{2,1,0:T(8,128)S(1)}, f32[2,112,128]{2,1,0:T(8,128)S(1)}, u32[]{:S(2)}, u32[]{:S(2)}) collective-permute-start(f32[2,112,128]{2,1,0:T(8,128)S(1)} %get-tuple-element.107), channel_id=1, source_target_pairs={{0,24},{4,28},{8,16},{12,20},{16,8},{20,12},{24,0},{28,4},{1,25},{... | collective-permute-start | bytes 344072 | tf_op jit(solution)/shard_map/ppermute | solution.py:349
  59.1 6.0 %collective-permute-start.13 = (f32[2,112,128]{2,1,0:T(8,128)S(1)}, f32[2,112,128]{2,1,0:T(8,128)S(1)}, u32[]{:S(2)}, u32[]{:S(2)}) collective-permute-start(f32[2,112,128]{2,1,0:T(8,128)S(1)} %shard_map.85.q0), channel_id=1, source_target_pairs={{0,8},{4,12},{8,0},{12,4},{16,24},{20,28},{24,16},{28,20},{1,9},{5... | collective-permute-start | bytes 344072 | tf_op jit(solution)/shard_map/ppermute | solution.py:349
  60.9 10.7 %collective-permute-start.14 = (f32[2,112,128]{2,1,0:T(8,128)S(1)}, f32[2,112,128]{2,1,0:T(8,128)S(1)}, u32[]{:S(2)}, u32[]{:S(2)}) collective-permute-start(f32[2,112,128]{2,1,0:T(8,128)S(1)} %shard_map.85.q0), channel_id=1, source_target_pairs={{0,16},{4,20},{8,24},{12,28},{16,0},{20,4},{24,8},{28,12},{1,17},{... | collective-permute-start | bytes 344072 | tf_op jit(solution)/shard_map/ppermute | solution.py:349
  62.0 9.6 %collective-permute-start.15 = (f32[2,112,128]{2,1,0:T(8,128)S(1)}, f32[2,112,128]{2,1,0:T(8,128)S(1)}, u32[]{:S(2)}, u32[]{:S(2)}) collective-permute-start(f32[2,112,128]{2,1,0:T(8,128)S(1)} %shard_map.85.q0), channel_id=1, source_target_pairs={{0,24},{4,28},{8,16},{12,20},{16,8},{20,12},{24,0},{28,4},{1,25},{... | collective-permute-start | bytes 344072 | tf_op jit(solution)/shard_map/ppermute | solution.py:349
  71.7 6.1 %collective-permute-start.16 = (f32[448,128]{1,0:T(8,128)S(1)}, f32[448,128]{1,0:T(8,128)S(1)}, u32[]{:S(2)}, u32[]{:S(2)}) collective-permute-start(f32[448,128]{1,0:T(8,128)S(1)} %get-tuple-element.108.own_a), channel_id=1, source_target_pairs={{0,4},{4,0},{8,12},{12,8},{16,20},{20,16},{24,28},{28,24},{1,5},{5... | collective-permute-start | bytes 688136 | tf_op jit(solution)/shard_map/ppermute | solution.py:349
  72.8 6.0 %collective-permute-start.17 = (f32[448,128]{1,0:T(8,128)S(1)}, f32[448,128]{1,0:T(8,128)S(1)}, u32[]{:S(2)}, u32[]{:S(2)}) collective-permute-start(f32[448,128]{1,0:T(8,128)S(1)} %get-tuple-element.109.own_b), channel_id=1, source_target_pairs={{0,2},{1,3},{2,0},{3,1},{4,6},{5,7},{6,4},{7,5},{8,10},{9,11},{10,... | collective-permute-start | bytes 688136 | tf_op jit(solution)/shard_map/ppermute | solution.py:349
  79.0 22.2 %collective-permute-start.22 = (f32[896,128]{1,0:T(8,128)S(1)}, f32[896,128]{1,0:T(8,128)S(1)}, u32[]{:S(2)}, u32[]{:S(2)}) collective-permute-start(f32[896,128]{1,0:T(8,128)S(1)} %get-tuple-element.110), channel_id=1, source_target_pairs={{0,1},{1,0},{2,3},{3,2},{4,5},{5,4},{6,7},{7,6},{8,9},{9,8},{10,11... | collective-permute-start | bytes 1376264 | tf_op jit(solution)/shard_map/ppermute | solution.py:349
  79.0 24.8 %collective-permute-start.23 = (f32[896,128]{1,0:T(8,128)S(1)}, f32[896,128]{1,0:T(8,128)S(1)}, u32[]{:S(2)}, u32[]{:S(2)}) collective-permute-start(f32[896,128]{1,0:T(8,128)S(1)} %get-tuple-element.111), channel_id=1, source_target_pairs={{0,1},{1,0},{2,3},{3,2},{4,5},{5,4},{6,7},{7,6},{8,9},{9,8},{10,11... | collective-permute-start | bytes 1376264 | tf_op jit(solution)/shard_map/ppermute | solution.py:349
  79.5 29.4 %collective-permute-start.18 = (f32[896,128]{1,0:T(8,128)S(1)}, f32[896,128]{1,0:T(8,128)S(1)}, u32[]{:S(2)}, u32[]{:S(2)}) collective-permute-start(f32[896,128]{1,0:T(8,128)S(1)} %get-tuple-element.110), channel_id=1, source_target_pairs={{0,2},{1,3},{2,0},{3,1},{4,6},{5,7},{6,4},{7,5},{8,10},{9,11},{10,... | collective-permute-start | bytes 1376264 | tf_op jit(solution)/shard_map/ppermute | solution.py:349
  81.4 27.5 %collective-permute-start.19 = (f32[896,128]{1,0:T(8,128)S(1)}, f32[896,128]{1,0:T(8,128)S(1)}, u32[]{:S(2)}, u32[]{:S(2)}) collective-permute-start(f32[896,128]{1,0:T(8,128)S(1)} %get-tuple-element.111), channel_id=1, source_target_pairs={{0,4},{4,0},{8,12},{12,8},{16,20},{20,16},{24,28},{28,24},{1,5},{5... | collective-permute-start | bytes 1376264 | tf_op jit(solution)/shard_map/ppermute | solution.py:349
  82.6 11.1 %collective-permute-start.20 = (f32[2,2,32,128]{3,2,1,0:T(8,128)S(1)}, f32[2,2,32,128]{3,2,1,0:T(8,128)S(1)}, u32[]{:S(2)}, u32[]{:S(2)}) collective-permute-start(f32[2,2,32,128]{3,2,1,0:T(8,128)S(1)} %get-tuple-element.112), channel_id=1, source_target_pairs={{0,4},{4,8},{8,12},{12,16},{16,20},{20,24},{24,28},{1,5},{5,9},{9,... | collective-permute-start | bytes 196616 | tf_op jit(solution)/shard_map/ppermute | solution.py:429
  93.8 6.6 %collective-permute-start.21 = (f32[2,2,32,128]{3,2,1,0:T(8,128)S(1)}, f32[2,2,32,128]{3,2,1,0:T(8,128)S(1)}, u32[]{:S(2)}, u32[]{:S(2)}) collective-permute-start(f32[2,2,32,128]{3,2,1,0:T(8,128)S(1)} %get-tuple-element.113), channel_id=1, source_target_pairs={{4,0},{8,4},{12,8},{16,12},{20,16},{24,20},{28,24},{5,1},{9,5},{13... | collective-permute-start | bytes 196616 | tf_op jit(solution)/shard_map/ppermute | solution.py:430
  100.4 4.8 %collective-permute-start.24 = (f32[2,6,32,128]{3,2,1,0:T(8,128)S(1)}, f32[2,6,32,128]{3,2,1,0:T(8,128)S(1)}, u32[]{:S(2)}, u32[]{:S(2)}) collective-permute-start(f32[2,6,32,128]{3,2,1,0:T(8,128)S(1)} %get-tuple-element.118), channel_id=1, source_target_pairs={{1,2},{2,1},{5,6},{6,5},{9,10},{10,9},{13,14},{14,13},{17,18},{18,... | collective-permute-start | bytes 589832 | tf_op jit(solution)/shard_map/ppermute | solution.py:441
  101.1 4.2 %collective-permute-start.25 = (f32[2,6,32,128]{3,2,1,0:T(8,128)S(1)}, f32[2,6,32,128]{3,2,1,0:T(8,128)S(1)}, u32[]{:S(2)}, u32[]{:S(2)}) collective-permute-start(f32[2,6,32,128]{3,2,1,0:T(8,128)S(1)} %get-tuple-element.119), channel_id=1, source_target_pairs={{0,1},{1,0},{2,3},{3,2},{4,5},{5,4},{6,7},{7,6},{8,9},{9,8},{10,11... | collective-permute-start | bytes 589832 | tf_op jit(solution)/shard_map/ppermute | solution.py:349
  103.9 1.4 %copy-start = (f32[4,2,32,128]{3,2,1,0:T(8,128)S(1)}, f32[4,2,32,128]{3,2,1,0:T(8,128)}, u32[]{:S(2)}) copy-start(f32[4,2,32,128]{3,2,1,0:T(8,128)} %clip.1) | copy-start | bytes 393220
  103.9 1.4 %copy-start.1 = (f32[4,2,32,128]{3,2,1,0:T(8,128)S(1)}, f32[4,2,32,128]{3,2,1,0:T(8,128)}, u32[]{:S(2)}) copy-start(f32[4,2,32,128]{3,2,1,0:T(8,128)} %cotangent.1) | copy-start | bytes 393220
  108.9 2.2 %collective-permute-start.26 = (f32[896,128]{1,0:T(8,128)S(1)}, f32[896,128]{1,0:T(8,128)S(1)}, u32[]{:S(2)}, u32[]{:S(2)}) collective-permute-start(f32[896,128]{1,0:T(8,128)S(1)} %collective-permute-done.18), channel_id=1, source_target_pairs={{0,1},{1,0},{2,3},{3,2},{4,5},{5,4},{6,7},{7,6},{8,9},{9,8},{10,11... | collective-permute-start | bytes 1376264 | tf_op jit(solution)/shard_map/ppermute | solution.py:349
  109.7 2.1 %collective-permute-start.27 = (f32[896,128]{1,0:T(8,128)S(1)}, f32[896,128]{1,0:T(8,128)S(1)}, u32[]{:S(2)}, u32[]{:S(2)}) collective-permute-start(f32[896,128]{1,0:T(8,128)S(1)} %collective-permute-done.19), channel_id=1, source_target_pairs={{0,1},{1,0},{2,3},{3,2},{4,5},{5,4},{6,7},{7,6},{8,9},{9,8},{10,11... | collective-permute-start | bytes 1376264 | tf_op jit(solution)/shard_map/ppermute | solution.py:349

commit v2 on v1

v2 whole, which is shorter than its diff:
```python
import math

import jax
import jax.numpy as jnp
from jax import lax
from jax.experimental import pallas as pl
from jax.experimental.pallas import tpu as pltpu
from jax.sharding import PartitionSpec as P

F32, BF16 = jnp.float32, jnp.bfloat16
VM, HBM = pltpu.VMEM, pltpu.HBM


def shaped(*dims, kind=F32):
    return jax.ShapeDtypeStruct(dims, kind)


def kernel(body, outs, args, scratch=(), flops=0, limit=20, far_in=(), far_out=(), alias=None):
    moved = sum(a.size * a.dtype.itemsize for a in (*args, *outs))
    args = [pltpu.with_memory_space_constraint(a, HBM) if i in far_in else a for i, a in enumerate(args)]
    return pl.pallas_call(
        body,
        out_shape=list(outs),
        in_specs=[pl.BlockSpec(memory_space=HBM if i in far_in else VM) for i in range(len(args))],
        out_specs=[pl.BlockSpec(memory_space=HBM if i in far_out else VM) for i in range(len(outs))],
        scratch_shapes=list(scratch),
        input_output_aliases=alias or {},
        compiler_params=pltpu.CompilerParams(vmem_limit_bytes=limit << 20),
        cost_estimate=pl.CostEstimate(flops=flops, bytes_accessed=moved, transcendentals=0),
    )(*args)


def halves(value):
    high = value.astype(BF16)
    return high, (value - high.astype(F32)).astype(BF16)


def moved_column(value, step, span):
    if step == 0:
        return value
    count = value.shape[0]
    column = lax.broadcasted_iota(jnp.int32, value.shape, 0) % span
    edge = span - 1 if step > 0 else 0
    return jnp.where(column == edge, 0.0, pltpu.roll(value, (-step) % count, 0))


def weights_body(plain, turned, *refs):
    count = max(0, len(refs) - 5)
    extra, (plain_out, turned_out), near = refs[:count], refs[count : count + 2], refs[count + 2 : -2]
    held, sem = refs[-2:]
    taps, ch = plain.shape[0], plain.shape[1]
    block = taps // 3
    copies = []
    for k in range(3):
        part = pl.ds(k * block, block)
        for which, source in enumerate((plain, turned)):
            copies.append(pltpu.make_async_copy(source.at[part], held.at[which, part], sem.at[which, k]))
    side = [pltpu.make_async_copy(a, near[0].at[k], sem.at[2, k]) for k, a in enumerate(extra)]
    for copy in (*copies, *side):
        copy.start()

    def step(tap, carry):
        high, low = halves(held[0, tap])
        plain_out[tap, :, 0:ch] = high
        plain_out[tap, :, ch : 2 * ch] = low
        high, low = halves(held[1, tap].T)
        turned_out[taps - 1 - tap, :, 0:ch] = high
        turned_out[taps - 1 - tap, :, ch : 2 * ch] = low
        return carry

    for k in range(3):
        copies[2 * k].wait()
        copies[2 * k + 1].wait()
        lax.fori_loop(k * block, (k + 1) * block, step, 0, unroll=True)
    for copy in side:
        copy.wait()


def weights(plain, turned, extra):
    taps, ch = plain.shape[0], plain.shape[1]
    out = shaped(taps, ch, 2 * ch, kind=BF16)
    return kernel(
        weights_body,
        [out, out] + [shaped(len(extra), *v.shape) for v in extra[:1]],
        (plain, turned, *extra),
        scratch=[pltpu.VMEM((2, taps, ch, ch), F32), pltpu.SemaphoreType.DMA((3, 3))],
        far_in=range(2 + len(extra)),
    )


def ends_body(first, second, tail, head, edge, sem):
    frames, depth, rows = first.shape[0], tail.shape[0], first.shape[1]
    row = (lax.axis_index("rows") % 2) * (rows - 1)
    pairs = (
        (first.at[pl.ds(frames - depth, depth)], tail),
        (second.at[pl.ds(0, depth)], head),
        (first.at[:, row], edge.at[0]),
        (second.at[:, row], edge.at[1]),
    )
    copies = [pltpu.make_async_copy(a, b, sem.at[k]) for k, (a, b) in enumerate(pairs)]
    for copy in copies:
        copy.start()
    for copy in copies:
        copy.wait()


def rim_body(before, after, halo, rim):
    odd = lax.axis_index("rows") % 2
    halo[0] = before[...]
    halo[1] = after[...]
    rim[...] = halo[:, :, odd * (before.shape[1] - 1)]


def pack_body(first, second, before, after, whole, outer, inner=None):
    frames = first.shape[0]
    depth = whole.shape[1] - frames
    lead = before.shape[0] - depth
    rows = first.shape[1]
    odd = lax.axis_index("rows") % 2
    whole[0, depth:] = first[...]
    whole[0, 0:depth] = before[lead:]
    whole[1, 0:frames] = second[...]
    whole[1, frames:] = after[0:depth]
    outer[...] = whole[:, :, odd * (rows - 1)]
    if inner is not None:
        inner[...] = whole[:, :, (1 - odd) * (rows - 1)]


def pack(first, second, before, after, edges):
    frames, rows, span, ch = first.shape
    edge = shaped(2, frames + 2, span, ch)
    return kernel(pack_body, [shaped(2, frames + 2, rows, span, ch)] + [edge] * edges, (first, second, before, after))


def convolve(strip, weight, shifted, columns, first=0, depth=3):
    tall, wide, span, ch = strip.shape
    frames, rows = tall - depth + 1, wide - 2
    cells = frames * rows * span
    flat = strip[...].reshape(tall * wide * span, ch)
    for c in range(3):
        high, low = halves(moved_column(flat, c - 1, span))
        shifted[0, c] = high.reshape(tall, wide, span, ch)
        shifted[1, c] = low.reshape(tall, wide, span, ch)
    for part in range(2):
        for a in range(depth):
            for b in range(3):
                for c in range(3):
                    tap = (a * 3 + b) * 3 + c
                    piece = shifted[part, c, a : a + frames, b : b + rows]
                    columns[part, :, tap * ch : (tap + 1) * ch] = piece.reshape(cells, ch)
    matrix = weight[9 * first : 9 * (first + depth)].reshape(9 * depth * ch, 2 * ch)
    main = jnp.dot(columns[0], matrix, preferred_element_type=F32)
    rest = jnp.dot(columns[1], matrix[:, :ch], preferred_element_type=F32)
    return main[:, :ch] + main[:, ch:] + rest


def conv_scratch(frames, rows, span, ch, depth=3):
    tall = frames + depth - 1
    return [
        pltpu.VMEM((tall, rows + 2, span, ch), F32),
        pltpu.VMEM((2, 3, tall, rows + 2, span, ch), BF16),
        pltpu.VMEM((2, frames * rows * span, 9 * depth * ch), BF16),
    ]


def place_rows(strip, own, outer, inner, odd):
    rows = own.shape[1]
    strip[:, 1 : rows + 1] = own
    strip[:, odd * (rows + 1)] = outer
    strip[:, (1 - odd) * (rows + 1)] = inner


def own_frames_body(own, outer, partner, w_one, w_two, pre, slope, *scratch):
    odd = lax.axis_index("rows") % 2
    frames, rows = own.shape[1:3]
    inner = odd * (rows - 1)
    for which, (weight, out) in enumerate(((w_one, pre), (w_two, slope))):
        strip, shifted, columns = scratch[3 * which : 3 * which + 3]
        lead = 2 - 2 * which
        place_rows(strip.at[lead : lead + frames], own[which], outer[which], partner[which, :, inner], odd)
        blank = frames * which
        strip[blank : blank + 2] = jnp.zeros((2, *strip.shape[1:]), F32)
        out[...] = convolve(strip, weight, shifted, columns)


def forward_body(pre_own, slope_own, halo, outer, partner, w_one, w_two, active, delta, tail, head, crossing, *scratch):
    odd = lax.axis_index("rows") % 2
    rows = halo.shape[2]
    inner = odd * (rows - 1)
    added = []
    for which, weight in enumerate((w_one, w_two)):
        strip, shifted, columns = scratch[3 * which : 3 * which + 3]
        place_rows(strip.at[which : which + 2], halo[which], outer[which], partner[which, :, inner], odd)
        strip[2 - 2 * which] = jnp.zeros(strip.shape[1:], F32)
        added.append(convolve(strip, weight, shifted, columns, which, 2))
    count = added[0].shape[0]
    rest = pre_own.shape[0] - count
    pre = jnp.concatenate([pre_own[:count] + added[0], pre_own[count:]], 0)
    slope = jnp.concatenate([slope_own[:rest], slope_own[rest:] + added[1]], 0)
    gate = jax.nn.sigmoid(pre)
    act = (pre * gate).reshape(active.shape)
    dlt = (slope * gate * (1.0 + pre * (1.0 - gate))).reshape(delta.shape)
    active[...] = act
    delta[...] = dlt
    tail[...] = act[active.shape[0] - 2 :]
    head[...] = dlt[:2]
    crossing[...] = jnp.where(odd == 0, dlt, act)


def outputs_body(ext, outer, inner, w_two, w_one, clip, cotangent, block_out, grad_clip, strip, shifted, columns):
    odd = lax.axis_index("rows") % 2
    place_rows(strip, ext[0], outer[0], inner[0], odd)
    block_out[...] = clip[...] + convolve(strip, w_two, shifted, columns).reshape(clip.shape)
    place_rows(strip, ext[1], outer[1], inner[1], odd)
    grad_clip[...] = cotangent[...] + convolve(strip, w_one, shifted, columns).reshape(clip.shape)


def bits_of():
    row = lax.axis_index("rows")
    return row % 2, (row // 2) % 2, lax.axis_index("tm") % 2


def turn(value, turned):
    ch = value.shape[-1]
    high, low = halves(value.reshape(-1, ch).T)
    turned[0:ch] = high
    turned[ch : 2 * ch] = low


def tap_sum(tap, turned, wide, frames, start, rows):
    a, b, c = tap // 9, (tap // 3) % 3, tap % 3
    ch = wide.shape[-1] // 2
    piece = wide[c, pl.ds(a, frames), pl.ds(b + start, rows)].reshape(-1, 2 * ch)
    product = jnp.dot(turned[...], piece, preferred_element_type=F32)
    left = product[:, :ch] + product[:, ch:]
    return left[:ch] + left[ch:]


def two_groups(first, second, side_a, side_b, block, sum_of, near=None):
    ch = block.shape[1]
    for j in range(7):
        rows = pl.ds(j * ch, ch)
        value = sum_of(side_a * 7 + j)
        first[rows] = value if near is None else near[0][rows] + value
        block[rows] = sum_of(14 + 6 * side_b + j)
    part = block[pl.ds(pl.multiple_of(side_b * (ch // 2), 8), second.shape[0])]
    second[...] = part if near is None else near[1][...] + part


def near_body(*refs):
    own_parts, (active, delta, wide, first, second, field, turned, block) = refs[:8], refs[8:]
    odd, y_bit, x_bit = bits_of()
    frames, rows, span, ch = active.shape
    tall = frames + 2
    pick = 1 - odd
    for part, (own, partner, outer, far) in enumerate((own_parts[:4], own_parts[4:])):
        span_of = pl.ds(frames * (1 - odd), 2) if part else pl.ds(2 * odd, frames)
        field[span_of, pl.ds(1 + rows * odd, rows)] = own[pick]
        field[span_of, pl.ds(1 + rows * (1 - odd), rows)] = partner[pick]
        field[span_of, odd * (2 * rows + 1)] = outer[pick]
        field[span_of, (1 - odd) * (2 * rows + 1)] = far[pick]
    flat = field[...].reshape(tall * (2 * rows + 2) * span, ch)
    for c in range(3):
        high, low = halves(moved_column(flat, c - 1, span))
        wide[c, :, :, :, 0:ch] = high.reshape(field.shape)
        wide[c, :, :, :, ch : 2 * ch] = low.reshape(field.shape)
    turn(jnp.where(odd == 0, active[...], delta[...]), turned)
    sum_of = lambda tap: tap_sum(tap, turned, wide, frames, rows * odd, rows)
    two_groups(first, second, 1 - y_bit, 1 - x_bit, block, sum_of)


def give_body(wide, near_a, near_b, arrived, first, second, turned, block):
    odd, y_bit, x_bit = bits_of()
    frames, rows = arrived.shape[:2]
    turn(arrived[...], turned)
    sum_of = lambda tap: tap_sum(tap, turned, wide, frames, rows * (1 - odd), rows)
    two_groups(first, second, 1 - y_bit, 1 - x_bit, block, sum_of, (near_a, near_b))


def keep_body(wide, active, delta, arrived, first, second, turned, block):
    odd, y_bit, x_bit = bits_of()
    frames, rows = arrived.shape[:2]
    mine = jnp.where(odd == 0, active[...], delta[...])
    other = arrived[...]
    upper = jnp.where(odd == 1, other, mine)
    lower = jnp.where(odd == 1, mine, other)
    turn(jnp.concatenate([upper, lower], 1), turned)
    sum_of = lambda tap: tap_sum(tap, turned, wide, frames, 0, 2 * rows)
    two_groups(first, second, y_bit, x_bit, block, sum_of)


def halve_body(keep_a, keep_b, got_a, got_b, stay_a, go_a, stay_b, go_b):
    x_bit = lax.axis_index("tm") % 2
    y_bit = (lax.axis_index("rows") // 2) % 2
    for keep, got, bit, stay, go in ((keep_a, got_a, x_bit, stay_a, go_a), (keep_b, got_b, y_bit, stay_b, go_b)):
        half = stay.shape[0]
        near = pl.ds(pl.multiple_of(bit * half, 8), half)
        away = pl.ds(pl.multiple_of((1 - bit) * half, 8), half)
        go[...] = keep[away] + got[away]
        stay[...] = keep[near] + got[near]


def quarter_body(keep_a, keep_b, got_a, got_b, *outs):
    z = (lax.axis_index("tm") // 2) % 4
    for d in range(4):
        start = 0
        for keep, got in ((keep_a, got_a), (keep_b, got_b)):
            size = keep.shape[0] // 4
            part = pl.ds(pl.multiple_of((z ^ d) * size, 8), size)
            outs[d][start : start + size] = keep[part] + got[part]
            start += size


def total_body(factor, *refs):
    *parts, out = refs
    value = parts[0][...]
    for part in parts[1:]:
        value = value + part[...]
    out[...] = value * factor


def join_quarters_body(q0, q1, q2, q3, out_a, out_b):
    z = (lax.axis_index("tm") // 2) % 4
    for d, quarter in enumerate((q0, q1, q2, q3)):
        start = 0
        for out in (out_a, out_b):
            size = out.shape[0] // 4
            out[pl.ds(pl.multiple_of((z ^ d) * size, 8), size)] = quarter[start : start + size]
            start += size


def join_halves_body(own_a, got_a, own_b, got_b, out_a, out_b):
    x_bit = lax.axis_index("tm") % 2
    y_bit = (lax.axis_index("rows") // 2) % 2
    for own, got, bit, out in ((own_a, got_a, x_bit, out_a), (own_b, got_b, y_bit, out_b)):
        half = own.shape[0]
        out[pl.ds(pl.multiple_of(bit * half, 8), half)] = own[...]
        out[pl.ds(pl.multiple_of((1 - bit) * half, 8), half)] = got[...]


def finish_body(late, foreign, *refs):
    first, second = refs[:2]
    one, two, turned, sem = refs[-4:]
    odd, y_bit, x_bit = bits_of()
    straight = odd == foreign
    side_a, side_b = y_bit ^ late, x_bit ^ late
    ch = one.shape[-1]
    half = ch // 2
    spots = [(first, pl.ds(j * ch, ch), side_a * 7 + j) for j in range(7)]
    spots += [(second, pl.ds(pl.multiple_of(side_b * half + j * ch, 8), ch), 14 + 7 * side_b + j) for j in range(6)]

    def shared(side):
        return pl.ds(pl.multiple_of((1 - side) * 6 * ch, 8), half)

    @pl.when(straight)
    def _():
        copies = [pltpu.make_async_copy(v.at[rows], two.at[26 - tap], sem.at[k]) for k, (v, rows, tap) in enumerate(spots)]
        place = pl.ds(pl.multiple_of(side_b * half, 8), half)
        copies.append(pltpu.make_async_copy(second.at[shared(side_b)], two.at[6, place], sem.at[13]))
        for copy in copies:
            copy.start()
        for copy in copies:
            copy.wait()

    @pl.when(jnp.logical_not(straight))
    def _():
        for k, (v, rows, _) in enumerate(spots):
            turned[k] = v[rows].T
        copies = [pltpu.make_async_copy(turned.at[k], one.at[tap], sem.at[k]) for k, (_, _, tap) in enumerate(spots)]
        if late:
            here, there = second[shared(side_b)], refs[2][shared(1 - side_b)]
            upper = jnp.where(side_b == 0, here, there)
            lower = jnp.where(side_b == 0, there, here)
            turned[13] = jnp.concatenate([upper, lower], 0).T
            copies.append(pltpu.make_async_copy(turned.at[13], one.at[20], sem.at[13]))
        for copy in copies:
            copy.start()
        for copy in copies:
            copy.wait()


def finish(late, foreign, sources, grads_so_far):
    ch = sources[0].shape[-1]
    grad = shaped(27, ch, ch)
    count = len(sources)
    return kernel(
        lambda *refs: finish_body(late, foreign, *refs),
        [grad, grad],
        [*sources, *grads_so_far],
        scratch=[pltpu.VMEM((14, ch, ch), F32), pltpu.SemaphoreType.DMA((14,))],
        far_in=(count, count + 1),
        far_out=(0, 1),
        alias={count: 0, count + 1: 1} if grads_so_far else None,
    )


def tied(*values):
    return list(lax.optimization_barrier(values))


def swapped(value, axis, bits):
    return lax.ppermute(value, axis, [(i, i ^ bits) for i in range(lax.axis_size(axis))])


def per_device(clip, kernel_one, kernel_two, cotangent):
    frames, rows, span, ch = clip.shape
    tm, strips = lax.axis_size("tm"), lax.axis_size("rows")
    factor = 1.0 / math.sqrt(frames * tm * rows * strips * span)
    later = [(i, i + 1) for i in range(tm - 1)]
    earlier = [(i + 1, i) for i in range(tm - 1)]
    across = [pair for i in range(1, strips - 1, 2) for pair in ((i, i + 1), (i + 1, i))]

    strip = shaped(2, rows, span, ch)
    cell = shaped(frames, rows, span, ch)
    tail, head, edge = kernel(
        ends_body,
        [strip, strip, shaped(2, frames, span, ch)],
        (clip, cotangent),
        scratch=[pltpu.SemaphoreType.DMA((4,))],
        far_in=(0, 1),
    )
    before = lax.ppermute(tail, "tm", later)
    after = lax.ppermute(head, "tm", earlier)
    outer = lax.ppermute(edge, "rows", across)
    one, two = kernel_one.reshape(27, ch, ch), kernel_two.reshape(27, ch, ch)
    one_plain, two_turned, own = weights(one, two, (clip, cotangent))
    partner = swapped(own, "rows", 1)
    before, after, one_plain, two_turned = tied(before, after, one_plain, two_turned)
    halo, rim = kernel(rim_body, [shaped(2, 2, rows, span, ch), shaped(2, 2, span, ch)], (before, after))
    outer_halo = lax.ppermute(rim, "rows", across)
    partner_halo = swapped(halo, "rows", 1)
    outer, partner, halo = tied(outer, partner, halo)
    far = swapped(outer, "rows", 1)

    conv_flops = 3 * 2 * frames * rows * span * 27 * ch * ch
    flat = shaped(frames * rows * span, ch)
    pre, slope = kernel(
        own_frames_body,
        [flat, flat],
        (own, outer, partner, one_plain, two_turned),
        scratch=conv_scratch(frames, rows, span, ch) * 2,
        flops=2 * conv_flops,
    )
    outer_halo, pre = tied(outer_halo, pre)
    far_halo = swapped(outer_halo, "rows", 1)
    active, delta, tail, head, crossing = kernel(
        forward_body,
        [cell, cell, strip, strip, cell],
        (pre, slope, halo, outer_halo, partner_halo, one_plain, two_turned),
        scratch=conv_scratch(2, rows, span, ch, 2) * 2,
        flops=conv_flops // 2,
    )
    arrived = swapped(crossing, "rows", 1)

    full = [shaped(7 * ch, ch), shaped(6 * ch + ch // 2, ch)]
    half, quarter = ([shaped(v.shape[0] // n, ch) for v in full] for n in (2, 8))
    quarter = shaped(quarter[0].shape[0] + quarter[1].shape[0], ch)
    block = pltpu.VMEM((7 * ch, ch), F32)
    tap_flops = 14 * 2 * (2 * ch) ** 2 * frames * rows * span
    far, active = tied(far, active)
    wide, near_a, near_b = kernel(
        near_body,
        [shaped(3, frames + 2, 2 * rows + 2, span, 2 * ch, kind=BF16), *full],
        (own, partner, outer, far, halo, partner_halo, outer_halo, far_halo, active, delta),
        scratch=[
            pltpu.VMEM((frames + 2, 2 * rows + 2, span, ch), F32),
            pltpu.VMEM((2 * ch, frames * rows * span), BF16),
            block,
        ],
        flops=tap_flops,
    )
    give_a, give_b = kernel(
        give_body,
        full,
        (wide, near_a, near_b, arrived),
        scratch=[pltpu.VMEM((2 * ch, frames * rows * span), BF16), block],
        flops=tap_flops,
    )
    got_a = swapped(give_a, "rows", 2)
    got_b = swapped(give_b, "tm", 1)
    keep_a, keep_b = kernel(
        keep_body,
        full,
        (wide, active, delta, arrived),
        scratch=[pltpu.VMEM((2 * ch, 2 * frames * rows * span), BF16), block],
        flops=2 * tap_flops,
    )
    keep_a, one, two = tied(keep_a, one, two)
    two_plain, one_turned = weights(two, one, ())
    keep_a, two_plain, one_turned = tied(keep_a, two_plain, one_turned)

    stay_a, go_a, stay_b, go_b = kernel(
        halve_body, [half[0], half[0], half[1], half[1]], (keep_a, keep_b, got_a, got_b)
    )
    got_a = swapped(go_a, "tm", 1)
    got_b = swapped(go_b, "rows", 2)
    parts = list(kernel(quarter_body, [quarter] * 4, (stay_a, stay_b, got_a, got_b)))
    summed = [parts[0]] + [swapped(parts[d], "tm", 2 * d) for d in range(1, 4)]

    before = lax.ppermute(tail, "tm", later)
    after = lax.ppermute(head, "tm", earlier)
    ext, edge, inside = pack(active, delta, before, after, 2)

    wider = [("tm", 1 << k) for k in range(3, tm.bit_length() - 1)]
    wider += [("rows", 1 << k) for k in range(2, strips.bit_length() - 1)]
    for axis, bits in wider:
        (shard,) = kernel(lambda *refs: total_body(1.0, *refs), [quarter], summed)
        summed = [shard, swapped(shard, axis, bits)]
    (shard,) = kernel(lambda *refs: total_body(factor, *refs), [quarter], summed)

    quarters = [shard] + [swapped(shard, "tm", 2 * d) for d in range(1, 4)]
    outer = lax.ppermute(edge, "rows", across)
    inner = swapped(inside, "rows", 1)
    own_a, own_b = kernel(join_quarters_body, half, quarters)
    got_a = swapped(own_a, "tm", 1)
    got_b = swapped(own_b, "rows", 2)
    own_a, outer, inner = tied(own_a, outer, inner)
    block_out, grad_clip = kernel(
        outputs_body,
        [cell, cell],
        (ext, outer, inner, two_plain, one_turned, clip, cotangent),
        scratch=conv_scratch(frames, rows, span, ch),
        flops=2 * conv_flops,
    )
    got_a, got_b, block_out, grad_clip = tied(got_a, got_b, block_out, grad_clip)
    mine = kernel(join_halves_body, full, (own_a, got_a, own_b, got_b))
    got = [swapped(mine[0], "rows", 2), swapped(mine[1], "tm", 1)]
    other = [swapped(v, "rows", 1) for v in mine]
    half_done = finish(0, 0, mine, ())
    half_done = list(finish(0, 1, other, half_done))
    got[0], got[1], *half_done = tied(*got, *half_done)
    got_other = [swapped(v, "rows", 1) for v in got]
    half_done = finish(1, 0, [*got, mine[1]], half_done)
    grad_one, grad_two = finish(1, 1, [*got_other, other[1]], half_done)
    shape = kernel_one.shape
    return block_out, grad_clip, grad_one.reshape(shape), grad_two.reshape(shape)


def solution(mesh):
    return jax.shard_map(
        per_device,
        mesh=mesh,
        in_specs=(P("tm", "rows", None, None), P(), P(), P("tm", "rows", None, None)),
        out_specs=(P("tm", "rows", None, None), P("tm", "rows", None, None), P(), P()),
        check_vma=False,
    )
```

time: 115 us -> 98.9 us (0.86); the launches traced: 113 us -> 98.6 us
  waiting for transfers between devices: 48.3 us -> 35.7 us
  starting transfers between devices: 43.5 us -> 40.5 us
    ppermute x2, waiting for transfers between devices: 8.4 us -> 0.59 us  [per_device(): before = lax.ppermute(tail, 'tm', later)]
    ppermute x2, waiting for transfers between devices: 7.85 us -> 4.28 us  [per_device(): after = lax.ppermute(head, 'tm', earlier)]
    ppermute x22 -> x24, starting transfers between devices: 32 us -> 28.8 us  [swapped(): lax.ppermute(value, axis, [(i, i ^ bits) for i in range(lax.axis_size(axi...]
    ppermute x22 -> x24, waiting for transfers between devices: 32.1 us -> 30.9 us  [swapped(): lax.ppermute(value, axis, [(i, i ^ bits) for i in range(lax.axis_size(axi...]
    pallas_call x19 -> x20, Pallas kernels: 20.4 us -> 21.3 us  [kernel(): pl.pallas_call(body, out_shape=list(outs), in_specs=[pl.BlockSpec(memory_...]
  transfers between devices with their start and end apart: 28 -> 31, of which waited for: 15 -> 10; matrix products, arithmetic and copies ran while one was open for 0% -> 0% of each run, Pallas kernels for 15% -> 17%
where the time goes in v2:
time: 98.9 us; the launch traced here: 98.6 us
  starting transfers between devices  40.5 us (41%)
  waiting for transfers between devices  35.7 us (36%)
  Pallas kernels  21.3 us (22%)
  between operations  1.06 us (1%)
    ppermute x24, waiting for transfers between devices, swapped(): lax.ppermute(value, axis, [(i, i ^ bits) for i in range(lax.axis_size(axi...  30.9 us
    ppermute x24, starting transfers between devices, swapped(): lax.ppermute(value, axis, [(i, i ^ bits) for i in range(lax.axis_size(axi...  28.8 us
    pallas_call x20, Pallas kernels, kernel(): pl.pallas_call(body, out_shape=list(outs), in_specs=[pl.BlockSpec(memory_...  21.3 us
    ppermute x2, starting transfers between devices, per_device(): before = lax.ppermute(tail, 'tm', later)  6.92 us
    ppermute x2, waiting for transfers between devices, per_device(): after = lax.ppermute(head, 'tm', earlier)  4.28 us
    ppermute x2, starting transfers between devices, per_device(): after = lax.ppermute(head, 'tm', earlier)  2.58 us
  transfers between devices with their start and end apart: 31, of which 10 were waited for; matrix products, arithmetic and copies ran while one was open for 0% of the time, Pallas kernels for 17%

profile of v2, /device:TPU:0, one launch (start us, length us, event | category | flops | bytes accessed | tf_op | source)
XLA Modules:
  0.0 98.6 jit_solution(5680758557837045831)
XLA Ops:
  0.6 2.3 %shard_map.75 = (bf16[27,128,256]{2,1,0:T(8,128)(2,1)S(1)}, bf16[27,128,256]{2,1,0:T(8,128)(2,1)S(1)}, f32[2,4,2,32,128]{4,3,2,1,0:T(8,128)S(1)}) custom-call(f32[27,128,128]{2,1,0:T(8,128)} %bitcast.6, f32[27,128,128]{2,1,0:T(8,128)} %bitcast.8, f32[4,2,32,128]{3,2,1,0:T(8,128)} %clip.1, f32[4,2,32,128]{3,2,1,0:T(8,128)} %cotangent.1), custom_call_target="tpu_custom_call" | custom-call | bytes 7602176 | tf_op jit(solution)/shard_map/pallas_call | solution.py:21
  5.2 4.4 %collective-permute-start.2 = (f32[2,2,32,128]{3,2,1,0:T(8,128)S(1)}, f32[2,2,32,128]{3,2,1,0:T(8,128)S(1)}, u32[]{:S(2)}, u32[]{:S(2)}) collective-permute-start(f32[2,2,32,128]{3,2,1,0:T(8,128)S(1)} %get-tuple-element.83), channel_id=1, source_target_pairs={{0,4},{4,8},{8,12},{12,16},{16,20},{20,24},{24,28},{1,5},{5,9},{9,... | collective-permute-start | bytes 196616 | tf_op jit(solution)/shard_map/ppermute | solution.py:422
  9.6 1.3 %collective-permute-start.3 = (f32[2,2,32,128]{3,2,1,0:T(8,128)S(1)}, f32[2,2,32,128]{3,2,1,0:T(8,128)S(1)}, u32[]{:S(2)}, u32[]{:S(2)}) collective-permute-start(f32[2,2,32,128]{3,2,1,0:T(8,128)S(1)} %get-tuple-element.84), channel_id=1, source_target_pairs={{4,0},{8,4},{12,8},{16,12},{20,16},{24,20},{28,24},{5,1},{9,5},{13... | collective-permute-start | bytes 196616 | tf_op jit(solution)/shard_map/ppermute | solution.py:423
  11.5 4.3 %collective-permute-done.3.after = f32[2,2,32,128]{3,2,1,0:T(8,128)S(1)} collective-permute-done((f32[2,2,32,128]{3,2,1,0:T(8,128)S(1)}, f32[2,2,32,128]{3,2,1,0:T(8,128)S(1)}, u32[]{:S(2)}, u32[]{:S(2)}) %collective-permute-start.3) | collective-permute-done | bytes 65568 | tf_op jit(solution)/shard_map/ppermute | solution.py:423
  15.8 1.5 %collective-permute-start.6 = (f32[2,2,2,32,128]{4,3,2,1,0:T(8,128)S(1)}, f32[2,2,2,32,128]{4,3,2,1,0:T(8,128)S(1)}, u32[]{:S(2)}, u32[]{:S(2)}) collective-permute-start(f32[2,2,2,32,128]{4,3,2,1,0:T(8,128)S(1)} %get-tuple-element.98.halo.refs_4_), channel_id=1, source_target_pairs={{0,1},{1,0},{2,3},{3,2},{4,5},{5,4},{6,7},{7,6},{8,9},{9,8},{10,11... | collective-permute-start | bytes 393224 | tf_op jit(solution)/shard_map/ppermute | solution.py:402
  17.9 3.4 %collective-permute-start.4 = (f32[2,4,32,128]{3,2,1,0:T(8,128)S(1)}, f32[2,4,32,128]{3,2,1,0:T(8,128)S(1)}, u32[]{:S(2)}, u32[]{:S(2)}) collective-permute-start(f32[2,4,32,128]{3,2,1,0:T(8,128)S(1)} %collective-permute-done.outer.refs_2_), channel_id=1, source_target_pairs={{0,1},{1,0},{2,3},{3,2},{4,5},{5,4},{6,7},{7,6},{8,9},{9,8},{10,11... | collective-permute-start | bytes 393224 | tf_op jit(solution)/shard_map/ppermute | solution.py:402
  21.3 2.5 %shard_map.78 = (f32[256,128]{1,0:T(8,128)S(1)}, f32[256,128]{1,0:T(8,128)S(1)}) custom-call(f32[2,4,2,32,128]{4,3,2,1,0:T(8,128)S(1)} %get-tuple-element.81.own.refs_0_, f32[2,4,32,128]{3,2,1,0:T(8,128)S(1)} %collective-permute-done.outer.refs_2_, f32[2,4,2,32,128]{4,3,2,1,0:T(8,128)S(1)} %collective-permute-done.1.partner.refs_1_, ...), custom_call_target="tpu_custom_call" | custom-call | flops 1358954496 | bytes 4456448 | tf_op jit(solution)/shard_map/pallas_call | solution.py:21
  26.3 1.5 %shard_map.80 = (bf16[3,6,6,32,256]{4,3,2,1,0:T(8,128)(2,1)S(1)}, f32[896,128]{1,0:T(8,128)S(1)}, f32[832,128]{1,0:T(8,128)S(1)}) custom-call(f32[2,4,2,32,128]{4,3,2,1,0:T(8,128)S(1)} %get-tuple-element.81.own.refs_0_, f32[2,4,2,32,128]{4,3,2,1,0:T(8,128)S(1)} %collective-permute-done.1.partner.refs_1_, ...), custom_call_target="tpu_custom_call" | custom-call | flops 469762048 | bytes 4096000 | tf_op jit(solution)/shard_map/pallas_call | solution.py:21
  28.6 1.1 %collective-permute-start.9 = (f32[896,128]{1,0:T(8,128)S(1)}, f32[896,128]{1,0:T(8,128)S(1)}, u32[]{:S(2)}, u32[]{:S(2)}) collective-permute-start(f32[896,128]{1,0:T(8,128)S(1)} %get-tuple-element.116), channel_id=1, source_target_pairs={{0,2},{1,3},{2,0},{3,1},{4,6},{5,7},{6,4},{7,5},{8,10},{9,11},{10,... | collective-permute-start | bytes 1376264 | tf_op jit(solution)/shard_map/ppermute | solution.py:402
  29.6 2.4 %collective-permute-start.10 = (f32[832,128]{1,0:T(8,128)S(1)}, f32[832,128]{1,0:T(8,128)S(1)}, u32[]{:S(2)}, u32[]{:S(2)}) collective-permute-start(f32[832,128]{1,0:T(8,128)S(1)} %get-tuple-element.117), channel_id=1, source_target_pairs={{0,4},{4,0},{8,12},{12,8},{16,20},{20,16},{24,28},{28,24},{1,5},{5... | collective-permute-start | bytes 1277960 | tf_op jit(solution)/shard_map/ppermute | solution.py:402
  32.1 1.2 %shard_map.81 = (f32[896,128]{1,0:T(8,128)S(1)}, f32[832,128]{1,0:T(8,128)S(1)}) custom-call(bf16[3,6,6,32,256]{4,3,2,1,0:T(8,128)(2,1)S(1)} %get-tuple-element.104.wide, f32[4,2,32,128]{3,2,1,0:T(8,128)S(1)} %get-tuple-element.102.refs_8_.active.first, f32[4,2,32,128]{3,2,1,0:T(8,128)S(1)} %get-tuple-element.103.refs_9_.delta.second, ...), custom_call_target="tpu_custom_call" | custom-call | flops 939524096 | bytes 3047424 | tf_op jit(solution)/shard_map/pallas_call | solution.py:21
  33.3 2.3 %shard_map.82 = (bf16[27,128,256]{2,1,0:T(8,128)(2,1)S(1)}, bf16[27,128,256]{2,1,0:T(8,128)(2,1)S(1)}) custom-call(f32[27,128,128]{2,1,0:T(8,128)} %bitcast.9, f32[27,128,128]{2,1,0:T(8,128)} %bitcast.7), custom_call_target="tpu_custom_call" | custom-call | bytes 7077888 | tf_op jit(solution)/shard_map/pallas_call | solution.py:21
  35.6 6.5 %collective-permute-done.10.got_b = f32[832,128]{1,0:T(8,128)S(1)} collective-permute-done((f32[832,128]{1,0:T(8,128)S(1)}, f32[832,128]{1,0:T(8,128)S(1)}, u32[]{:S(2)}, u32[]{:S(2)}) %collective-permute-start.10) | collective-permute-done | bytes 426016 | tf_op jit(solution)/shard_map/ppermute | solution.py:402
  42.2 1.8 %collective-permute-start.11 = (f32[448,128]{1,0:T(8,128)S(1)}, f32[448,128]{1,0:T(8,128)S(1)}, u32[]{:S(2)}, u32[]{:S(2)}) collective-permute-start(f32[448,128]{1,0:T(8,128)S(1)} %get-tuple-element.120), channel_id=1, source_target_pairs={{0,4},{4,0},{8,12},{12,8},{16,20},{20,16},{24,28},{28,24},{1,5},{5... | collective-permute-start | bytes 688136 | tf_op jit(solution)/shard_map/ppermute | solution.py:402
  44.0 1.0 %collective-permute-start.12 = (f32[416,128]{1,0:T(8,128)S(1)}, f32[416,128]{1,0:T(8,128)S(1)}, u32[]{:S(2)}, u32[]{:S(2)}) collective-permute-start(f32[416,128]{1,0:T(8,128)S(1)} %get-tuple-element.121), channel_id=1, source_target_pairs={{0,2},{1,3},{2,0},{3,1},{4,6},{5,7},{6,4},{7,5},{8,10},{9,11},{10,... | collective-permute-start | bytes 638984 | tf_op jit(solution)/shard_map/ppermute | solution.py:402
  45.1 5.3 %collective-permute-done.12.got_b = f32[416,128]{1,0:T(8,128)S(1)} collective-permute-done((f32[416,128]{1,0:T(8,128)S(1)}, f32[416,128]{1,0:T(8,128)S(1)}, u32[]{:S(2)}, u32[]{:S(2)}) %collective-permute-start.12) | collective-permute-done | bytes 213024 | tf_op jit(solution)/shard_map/ppermute | solution.py:402
  50.4 1.7 %collective-permute-start.13 = (f32[216,128]{1,0:T(8,128)S(1)}, f32[216,128]{1,0:T(8,128)S(1)}, u32[]{:S(2)}, u32[]{:S(2)}) collective-permute-start(f32[216,128]{1,0:T(8,128)S(1)} %get-tuple-element.123), channel_id=1, source_target_pairs={{0,8},{4,12},{8,0},{12,4},{16,24},{20,28},{24,16},{28,20},{1,9},{5... | collective-permute-start | bytes 331784 | tf_op jit(solution)/shard_map/ppermute | solution.py:402
  52.1 1.1 %collective-permute-start.14 = (f32[216,128]{1,0:T(8,128)S(1)}, f32[216,128]{1,0:T(8,128)S(1)}, u32[]{:S(2)}, u32[]{:S(2)}) collective-permute-start(f32[216,128]{1,0:T(8,128)S(1)} %get-tuple-element.124), channel_id=1, source_target_pairs={{0,16},{4,20},{8,24},{12,28},{16,0},{20,4},{24,8},{28,12},{1,17},{... | collective-permute-start | bytes 331784 | tf_op jit(solution)/shard_map/ppermute | solution.py:402
  53.1 1.7 %collective-permute-start.15 = (f32[216,128]{1,0:T(8,128)S(1)}, f32[216,128]{1,0:T(8,128)S(1)}, u32[]{:S(2)}, u32[]{:S(2)}) collective-permute-start(f32[216,128]{1,0:T(8,128)S(1)} %get-tuple-element.125), channel_id=1, source_target_pairs={{0,24},{4,28},{8,16},{12,20},{16,8},{20,12},{24,0},{28,4},{1,25},{... | collective-permute-start | bytes 331784 | tf_op jit(solution)/shard_map/ppermute | solution.py:402
  54.9 2.5 %collective-permute-start.21 = (f32[2,2,32,128]{3,2,1,0:T(8,128)S(1)}, f32[2,2,32,128]{3,2,1,0:T(8,128)S(1)}, u32[]{:S(2)}, u32[]{:S(2)}) collective-permute-start(f32[2,2,32,128]{3,2,1,0:T(8,128)S(1)} %get-tuple-element.128), channel_id=1, source_target_pairs={{0,4},{4,8},{8,12},{12,16},{16,20},{20,24},{24,28},{1,5},{5,9},{9,... | collective-permute-start | bytes 196616 | tf_op jit(solution)/shard_map/ppermute | solution.py:500
  57.4 1.3 %collective-permute-start.22 = (f32[2,2,32,128]{3,2,1,0:T(8,128)S(1)}, f32[2,2,32,128]{3,2,1,0:T(8,128)S(1)}, u32[]{:S(2)}, u32[]{:S(2)}) collective-permute-start(f32[2,2,32,128]{3,2,1,0:T(8,128)S(1)} %get-tuple-element.129), channel_id=1, source_target_pairs={{4,0},{8,4},{12,8},{16,12},{20,16},{24,20},{28,24},{5,1},{9,5},{13... | collective-permute-start | bytes 196616 | tf_op jit(solution)/shard_map/ppermute | solution.py:501
  58.7 3.3 %collective-permute-done.14.refs_2_ = f32[216,128]{1,0:T(8,128)S(1)} collective-permute-done((f32[216,128]{1,0:T(8,128)S(1)}, f32[216,128]{1,0:T(8,128)S(1)}, u32[]{:S(2)}, u32[]{:S(2)}) %collective-permute-start.14) | collective-permute-done | bytes 110624 | tf_op jit(solution)/shard_map/ppermute | solution.py:402
  62.0 2.4 %collective-permute-start.16 = (f32[216,128]{1,0:T(8,128)S(1)}, f32[216,128]{1,0:T(8,128)S(1)}, u32[]{:S(2)}, u32[]{:S(2)}) collective-permute-start(f32[216,128]{1,0:T(8,128)S(1)} %shard_map.86.q0), channel_id=1, source_target_pairs={{0,8},{4,12},{8,0},{12,4},{16,24},{20,28},{24,16},{28,20},{1,9},{5... | collective-permute-start | bytes 331784 | tf_op jit(solution)/shard_map/ppermute | solution.py:402
  64.7 2.1 %collective-permute-start.18 = (f32[216,128]{1,0:T(8,128)S(1)}, f32[216,128]{1,0:T(8,128)S(1)}, u32[]{:S(2)}, u32[]{:S(2)}) collective-permute-start(f32[216,128]{1,0:T(8,128)S(1)} %shard_map.86.q0), channel_id=1, source_target_pairs={{0,24},{4,28},{8,16},{12,20},{16,8},{20,12},{24,0},{28,4},{1,25},{... | collective-permute-start | bytes 331784 | tf_op jit(solution)/shard_map/ppermute | solution.py:402
  67.8 2.4 %collective-permute-start.24 = (f32[2,6,32,128]{3,2,1,0:T(8,128)S(1)}, f32[2,6,32,128]{3,2,1,0:T(8,128)S(1)}, u32[]{:S(2)}, u32[]{:S(2)}) collective-permute-start(f32[2,6,32,128]{3,2,1,0:T(8,128)S(1)} %get-tuple-element.132), channel_id=1, source_target_pairs={{0,1},{1,0},{2,3},{3,2},{4,5},{5,4},{6,7},{7,6},{8,9},{9,8},{10,11... | collective-permute-start | bytes 589832 | tf_op jit(solution)/shard_map/ppermute | solution.py:402
  70.1 4.2 %collective-permute-done.17.q2 = f32[216,128]{1,0:T(8,128)S(1)} collective-permute-done((f32[216,128]{1,0:T(8,128)S(1)}, f32[216,128]{1,0:T(8,128)S(1)}, u32[]{:S(2)}, u32[]{:S(2)}) %collective-permute-start.17) | collective-permute-done | bytes 110624 | tf_op jit(solution)/shard_map/ppermute | solution.py:402
  76.4 3.6 %shard_map.89 = (f32[4,2,32,128]{3,2,1,0:T(8,128)}, f32[4,2,32,128]{3,2,1,0:T(8,128)}) custom-call(f32[2,6,2,32,128]{4,3,2,1,0:T(8,128)S(1)} %get-tuple-element.130.ext, f32[2,6,32,128]{3,2,1,0:T(8,128)S(1)} %collective-permute-done.23.outer, f32[2,6,32,128]{3,2,1,0:T(8,128)S(1)} %collective-permute-done.24.inner, ...), custom_call_target="tpu_custom_call" | custom-call | flops 1358954496 | bytes 4849664 | tf_op jit(solution)/shard_map/pallas_call | solution.py:21
  80.0 1.2 %collective-permute-done.20.got_b = f32[416,128]{1,0:T(8,128)S(1)} collective-permute-done((f32[416,128]{1,0:T(8,128)S(1)}, f32[416,128]{1,0:T(8,128)S(1)}, u32[]{:S(2)}, u32[]{:S(2)}) %collective-permute-start.20) | collective-permute-done | bytes 213024 | tf_op jit(solution)/shard_map/ppermute | solution.py:402
  82.6 1.1 %collective-permute-start.26 = (f32[832,128]{1,0:T(8,128)S(1)}, f32[832,128]{1,0:T(8,128)S(1)}, u32[]{:S(2)}, u32[]{:S(2)}) collective-permute-start(f32[832,128]{1,0:T(8,128)S(1)} %get-tuple-element.145.refs_1_.refs_2_), channel_id=1, source_target_pairs={{0,4},{4,0},{8,12},{12,8},{16,20},{20,16},{24,28},{28,24},{1,5},{5... | collective-permute-start | bytes 1277960 | tf_op jit(solution)/shard_map/ppermute | solution.py:402
  84.7 1.4 %shard_map.92 = (f32[27,128,128]{2,1,0:T(8,128)}, f32[27,128,128]{2,1,0:T(8,128)}) custom-call(f32[896,128]{1,0:T(8,128)S(1)} %collective-permute-done.27.refs_0_, f32[832,128]{1,0:T(8,128)S(1)} %collective-permute-done.28.refs_1_.refs_2_, f32[27,128,128]{2,1,0:T(8,128)} %get-tuple-element.146.refs_2_, ...), custom_call_target="tpu_custom_call", output_to_operand_aliasing={{0}: (2, {}), {1}: (3, {})} | custom-call | bytes 7962624 | tf_op jit(solution)/shard_map/pallas_call | solution.py:21
  86.1 8.5 %collective-permute-done.26.refs_1_ = f32[832,128]{1,0:T(8,128)S(1)} collective-permute-done((f32[832,128]{1,0:T(8,128)S(1)}, f32[832,128]{1,0:T(8,128)S(1)}, u32[]{:S(2)}, u32[]{:S(2)}) %collective-permute-start.26) | collective-permute-done | bytes 426016 | tf_op jit(solution)/shard_map/ppermute | solution.py:402
  97.1 1.3 %shard_map.94 = (f32[27,128,128]{2,1,0:T(8,128)}, f32[27,128,128]{2,1,0:T(8,128)}) custom-call(f32[896,128]{1,0:T(8,128)S(1)} %collective-permute-done.29.refs_0_, f32[832,128]{1,0:T(8,128)S(1)} %collective-permute-done.30.refs_1_, f32[832,128]{1,0:T(8,128)S(1)} %collective-permute-done.28.refs_1_.refs_2_, ...), custom_call_target="tpu_custom_call", output_to_operand_aliasing={{0}: (3, {}), {1}: (4, {})} | custom-call | bytes 8388608 | tf_op jit(solution)/shard_map/pallas_call | solution.py:21
  (54 shorter events, 14.9 us)
Async XLA Ops:
  3.0 15.0 %collective-permute-start.1 = (f32[2,4,2,32,128]{4,3,2,1,0:T(8,128)S(1)}, f32[2,4,2,32,128]{4,3,2,1,0:T(8,128)S(1)}, u32[]{:S(2)}, u32[]{:S(2)}) collective-permute-start(f32[2,4,2,32,128]{4,3,2,1,0:T(8,128)S(1)} %get-tuple-element.81.own.refs_0_), channel_id=1, source_target_pairs={{0,1},{1,0},{2,3},{3,2},{4,5},{5,4},{6,7},{7,6},{8,9},{9,8},{10,11... | collective-permute-start | bytes 786440 | tf_op jit(solution)/shard_map/ppermute | solution.py:402
  4.5 13.4 %collective-permute-start = (f32[2,4,32,128]{3,2,1,0:T(8,128)S(1)}, f32[2,4,32,128]{3,2,1,0:T(8,128)S(1)}, u32[]{:S(2)}, u32[]{:S(2)}) collective-permute-start(f32[2,4,32,128]{3,2,1,0:T(8,128)S(1)} %get-tuple-element.82), channel_id=1, source_target_pairs={{1,2},{2,1},{5,6},{6,5},{9,10},{10,9},{13,14},{14,13},{17,18},{18,... | collective-permute-start | bytes 393224 | tf_op jit(solution)/shard_map/ppermute | solution.py:424
  5.2 6.3 %collective-permute-start.2 = (f32[2,2,32,128]{3,2,1,0:T(8,128)S(1)}, f32[2,2,32,128]{3,2,1,0:T(8,128)S(1)}, u32[]{:S(2)}, u32[]{:S(2)}) collective-permute-start(f32[2,2,32,128]{3,2,1,0:T(8,128)S(1)} %get-tuple-element.83), channel_id=1, source_target_pairs={{0,4},{4,8},{8,12},{12,16},{16,20},{20,24},{24,28},{1,5},{5,9},{9,... | collective-permute-start | bytes 196616 | tf_op jit(solution)/shard_map/ppermute | solution.py:422
  9.6 6.2 %collective-permute-start.3 = (f32[2,2,32,128]{3,2,1,0:T(8,128)S(1)}, f32[2,2,32,128]{3,2,1,0:T(8,128)S(1)}, u32[]{:S(2)}, u32[]{:S(2)}) collective-permute-start(f32[2,2,32,128]{3,2,1,0:T(8,128)S(1)} %get-tuple-element.84), channel_id=1, source_target_pairs={{4,0},{8,4},{12,8},{16,12},{20,16},{24,20},{28,24},{5,1},{9,5},{13... | collective-permute-start | bytes 196616 | tf_op jit(solution)/shard_map/ppermute | solution.py:423
  15.8 8.0 %collective-permute-start.6 = (f32[2,2,2,32,128]{4,3,2,1,0:T(8,128)S(1)}, f32[2,2,2,32,128]{4,3,2,1,0:T(8,128)S(1)}, u32[]{:S(2)}, u32[]{:S(2)}) collective-permute-start(f32[2,2,2,32,128]{4,3,2,1,0:T(8,128)S(1)} %get-tuple-element.98.halo.refs_4_), channel_id=1, source_target_pairs={{0,1},{1,0},{2,3},{3,2},{4,5},{5,4},{6,7},{7,6},{8,9},{9,8},{10,11... | collective-permute-start | bytes 393224 | tf_op jit(solution)/shard_map/ppermute | solution.py:402
  17.3 6.5 %collective-permute-start.5 = (f32[2,2,32,128]{3,2,1,0:T(8,128)S(1)}, f32[2,2,32,128]{3,2,1,0:T(8,128)S(1)}, u32[]{:S(2)}, u32[]{:S(2)}) collective-permute-start(f32[2,2,32,128]{3,2,1,0:T(8,128)S(1)} %get-tuple-element.92), channel_id=1, source_target_pairs={{1,2},{2,1},{5,6},{6,5},{9,10},{10,9},{13,14},{14,13},{17,18},{18,... | collective-permute-start | bytes 196616 | tf_op jit(solution)/shard_map/ppermute | solution.py:430
  17.9 7.4 %collective-permute-start.4 = (f32[2,4,32,128]{3,2,1,0:T(8,128)S(1)}, f32[2,4,32,128]{3,2,1,0:T(8,128)S(1)}, u32[]{:S(2)}, u32[]{:S(2)}) collective-permute-start(f32[2,4,32,128]{3,2,1,0:T(8,128)S(1)} %collective-permute-done.outer.refs_2_), channel_id=1, source_target_pairs={{0,1},{1,0},{2,3},{3,2},{4,5},{5,4},{6,7},{7,6},{8,9},{9,8},{10,11... | collective-permute-start | bytes 393224 | tf_op jit(solution)/shard_map/ppermute | solution.py:402
  24.8 3.0 %collective-permute-start.8 = (f32[4,2,32,128]{3,2,1,0:T(8,128)S(1)}, f32[4,2,32,128]{3,2,1,0:T(8,128)S(1)}, u32[]{:S(2)}, u32[]{:S(2)}) collective-permute-start(f32[4,2,32,128]{3,2,1,0:T(8,128)S(1)} %get-tuple-element.105), channel_id=1, source_target_pairs={{0,1},{1,0},{2,3},{3,2},{4,5},{5,4},{6,7},{7,6},{8,9},{9,8},{10,11... | collective-permute-start | bytes 393224 | tf_op jit(solution)/shard_map/ppermute | solution.py:402
  24.8 1.4 %collective-permute-start.7 = (f32[2,2,32,128]{3,2,1,0:T(8,128)S(1)}, f32[2,2,32,128]{3,2,1,0:T(8,128)S(1)}, u32[]{:S(2)}, u32[]{:S(2)}) collective-permute-start(f32[2,2,32,128]{3,2,1,0:T(8,128)S(1)} %collective-permute-done.5.outer.refs_6_), channel_id=1, source_target_pairs={{0,1},{1,0},{2,3},{3,2},{4,5},{5,4},{6,7},{7,6},{8,9},{9,8},{10,11... | collective-permute-start | bytes 196616 | tf_op jit(solution)/shard_map/ppermute | solution.py:402
  28.6 13.5 %collective-permute-start.9 = (f32[896,128]{1,0:T(8,128)S(1)}, f32[896,128]{1,0:T(8,128)S(1)}, u32[]{:S(2)}, u32[]{:S(2)}) collective-permute-start(f32[896,128]{1,0:T(8,128)S(1)} %get-tuple-element.116), channel_id=1, source_target_pairs={{0,2},{1,3},{2,0},{3,1},{4,6},{5,7},{6,4},{7,5},{8,10},{9,11},{10,... | collective-permute-start | bytes 1376264 | tf_op jit(solution)/shard_map/ppermute | solution.py:402
  29.6 12.5 %collective-permute-start.10 = (f32[832,128]{1,0:T(8,128)S(1)}, f32[832,128]{1,0:T(8,128)S(1)}, u32[]{:S(2)}, u32[]{:S(2)}) collective-permute-start(f32[832,128]{1,0:T(8,128)S(1)} %get-tuple-element.117), channel_id=1, source_target_pairs={{0,4},{4,0},{8,12},{12,8},{16,20},{20,16},{24,28},{28,24},{1,5},{5... | collective-permute-start | bytes 1277960 | tf_op jit(solution)/shard_map/ppermute | solution.py:402
  42.1 34.2 %copy-start.1 = (f32[4,2,32,128]{3,2,1,0:T(8,128)S(1)}, f32[4,2,32,128]{3,2,1,0:T(8,128)}, u32[]{:S(2)}) copy-start(f32[4,2,32,128]{3,2,1,0:T(8,128)} %cotangent.1) | copy-start | bytes 393220
  42.2 8.1 %collective-permute-start.11 = (f32[448,128]{1,0:T(8,128)S(1)}, f32[448,128]{1,0:T(8,128)S(1)}, u32[]{:S(2)}, u32[]{:S(2)}) collective-permute-start(f32[448,128]{1,0:T(8,128)S(1)} %get-tuple-element.120), channel_id=1, source_target_pairs={{0,4},{4,0},{8,12},{12,8},{16,20},{20,16},{24,28},{28,24},{1,5},{5... | collective-permute-start | bytes 688136 | tf_op jit(solution)/shard_map/ppermute | solution.py:402
  44.0 6.3 %collective-permute-start.12 = (f32[416,128]{1,0:T(8,128)S(1)}, f32[416,128]{1,0:T(8,128)S(1)}, u32[]{:S(2)}, u32[]{:S(2)}) collective-permute-start(f32[416,128]{1,0:T(8,128)S(1)} %get-tuple-element.121), channel_id=1, source_target_pairs={{0,2},{1,3},{2,0},{3,1},{4,6},{5,7},{6,4},{7,5},{8,10},{9,11},{10,... | collective-permute-start | bytes 638984 | tf_op jit(solution)/shard_map/ppermute | solution.py:402
  50.4 8.3 %collective-permute-start.13 = (f32[216,128]{1,0:T(8,128)S(1)}, f32[216,128]{1,0:T(8,128)S(1)}, u32[]{:S(2)}, u32[]{:S(2)}) collective-permute-start(f32[216,128]{1,0:T(8,128)S(1)} %get-tuple-element.123), channel_id=1, source_target_pairs={{0,8},{4,12},{8,0},{12,4},{16,24},{20,28},{24,16},{28,20},{1,9},{5... | collective-permute-start | bytes 331784 | tf_op jit(solution)/shard_map/ppermute | solution.py:402
  52.1 9.9 %collective-permute-start.14 = (f32[216,128]{1,0:T(8,128)S(1)}, f32[216,128]{1,0:T(8,128)S(1)}, u32[]{:S(2)}, u32[]{:S(2)}) collective-permute-start(f32[216,128]{1,0:T(8,128)S(1)} %get-tuple-element.124), channel_id=1, source_target_pairs={{0,16},{4,20},{8,24},{12,28},{16,0},{20,4},{24,8},{28,12},{1,17},{... | collective-permute-start | bytes 331784 | tf_op jit(solution)/shard_map/ppermute | solution.py:402
  53.1 8.8 %collective-permute-start.15 = (f32[216,128]{1,0:T(8,128)S(1)}, f32[216,128]{1,0:T(8,128)S(1)}, u32[]{:S(2)}, u32[]{:S(2)}) collective-permute-start(f32[216,128]{1,0:T(8,128)S(1)} %get-tuple-element.125), channel_id=1, source_target_pairs={{0,24},{4,28},{8,16},{12,20},{16,8},{20,12},{24,0},{28,4},{1,25},{... | collective-permute-start | bytes 331784 | tf_op jit(solution)/shard_map/ppermute | solution.py:402
  54.9 12.0 %collective-permute-start.21 = (f32[2,2,32,128]{3,2,1,0:T(8,128)S(1)}, f32[2,2,32,128]{3,2,1,0:T(8,128)S(1)}, u32[]{:S(2)}, u32[]{:S(2)}) collective-permute-start(f32[2,2,32,128]{3,2,1,0:T(8,128)S(1)} %get-tuple-element.128), channel_id=1, source_target_pairs={{0,4},{4,8},{8,12},{12,16},{16,20},{20,24},{24,28},{1,5},{5,9},{9,... | collective-permute-start | bytes 196616 | tf_op jit(solution)/shard_map/ppermute | solution.py:500
  57.4 9.5 %collective-permute-start.22 = (f32[2,2,32,128]{3,2,1,0:T(8,128)S(1)}, f32[2,2,32,128]{3,2,1,0:T(8,128)S(1)}, u32[]{:S(2)}, u32[]{:S(2)}) collective-permute-start(f32[2,2,32,128]{3,2,1,0:T(8,128)S(1)} %get-tuple-element.129), channel_id=1, source_target_pairs={{4,0},{8,4},{12,8},{16,12},{20,16},{24,20},{28,24},{5,1},{9,5},{13... | collective-permute-start | bytes 196616 | tf_op jit(solution)/shard_map/ppermute | solution.py:501
  62.0 8.1 %collective-permute-start.16 = (f32[216,128]{1,0:T(8,128)S(1)}, f32[216,128]{1,0:T(8,128)S(1)}, u32[]{:S(2)}, u32[]{:S(2)}) collective-permute-start(f32[216,128]{1,0:T(8,128)S(1)} %shard_map.86.q0), channel_id=1, source_target_pairs={{0,8},{4,12},{8,0},{12,4},{16,24},{20,28},{24,16},{28,20},{1,9},{5... | collective-permute-start | bytes 331784 | tf_op jit(solution)/shard_map/ppermute | solution.py:402
  64.4 9.9 %collective-permute-start.17 = (f32[216,128]{1,0:T(8,128)S(1)}, f32[216,128]{1,0:T(8,128)S(1)}, u32[]{:S(2)}, u32[]{:S(2)}) collective-permute-start(f32[216,128]{1,0:T(8,128)S(1)} %shard_map.86.q0), channel_id=1, source_target_pairs={{0,16},{4,20},{8,24},{12,28},{16,0},{20,4},{24,8},{28,12},{1,17},{... | collective-permute-start | bytes 331784 | tf_op jit(solution)/shard_map/ppermute | solution.py:402
  64.7 9.6 %collective-permute-start.18 = (f32[216,128]{1,0:T(8,128)S(1)}, f32[216,128]{1,0:T(8,128)S(1)}, u32[]{:S(2)}, u32[]{:S(2)}) collective-permute-start(f32[216,128]{1,0:T(8,128)S(1)} %shard_map.86.q0), channel_id=1, source_target_pairs={{0,24},{4,28},{8,16},{12,20},{16,8},{20,12},{24,0},{28,4},{1,25},{... | collective-permute-start | bytes 331784 | tf_op jit(solution)/shard_map/ppermute | solution.py:402
  66.9 9.4 %collective-permute-start.23 = (f32[2,6,32,128]{3,2,1,0:T(8,128)S(1)}, f32[2,6,32,128]{3,2,1,0:T(8,128)S(1)}, u32[]{:S(2)}, u32[]{:S(2)}) collective-permute-start(f32[2,6,32,128]{3,2,1,0:T(8,128)S(1)} %get-tuple-element.131), channel_id=1, source_target_pairs={{1,2},{2,1},{5,6},{6,5},{9,10},{10,9},{13,14},{14,13},{17,18},{18,... | collective-permute-start | bytes 589832 | tf_op jit(solution)/shard_map/ppermute | solution.py:512
  67.8 8.6 %collective-permute-start.24 = (f32[2,6,32,128]{3,2,1,0:T(8,128)S(1)}, f32[2,6,32,128]{3,2,1,0:T(8,128)S(1)}, u32[]{:S(2)}, u32[]{:S(2)}) collective-permute-start(f32[2,6,32,128]{3,2,1,0:T(8,128)S(1)} %get-tuple-element.132), channel_id=1, source_target_pairs={{0,1},{1,0},{2,3},{3,2},{4,5},{5,4},{6,7},{7,6},{8,9},{9,8},{10,11... | collective-permute-start | bytes 589832 | tf_op jit(solution)/shard_map/ppermute | solution.py:402
  74.4 6.8 %collective-permute-start.19 = (f32[448,128]{1,0:T(8,128)S(1)}, f32[448,128]{1,0:T(8,128)S(1)}, u32[]{:S(2)}, u32[]{:S(2)}) collective-permute-start(f32[448,128]{1,0:T(8,128)S(1)} %get-tuple-element.141.own_a), channel_id=1, source_target_pairs={{0,4},{4,0},{8,12},{12,8},{16,20},{20,16},{24,28},{28,24},{1,5},{5... | collective-permute-start | bytes 688136 | tf_op jit(solution)/shard_map/ppermute | solution.py:402
  75.4 5.8 %collective-permute-start.20 = (f32[416,128]{1,0:T(8,128)S(1)}, f32[416,128]{1,0:T(8,128)S(1)}, u32[]{:S(2)}, u32[]{:S(2)}) collective-permute-start(f32[416,128]{1,0:T(8,128)S(1)} %get-tuple-element.127.own_b), channel_id=1, source_target_pairs={{0,2},{1,3},{2,0},{3,1},{4,6},{5,7},{6,4},{7,5},{8,10},{9,11},{10,... | collective-permute-start | bytes 638984 | tf_op jit(solution)/shard_map/ppermute | solution.py:402
  81.3 3.4 %collective-permute-start.27 = (f32[896,128]{1,0:T(8,128)S(1)}, f32[896,128]{1,0:T(8,128)S(1)}, u32[]{:S(2)}, u32[]{:S(2)}) collective-permute-start(f32[896,128]{1,0:T(8,128)S(1)} %get-tuple-element.144.refs_0_), channel_id=1, source_target_pairs={{0,1},{1,0},{2,3},{3,2},{4,5},{5,4},{6,7},{7,6},{8,9},{9,8},{10,11... | collective-permute-start | bytes 1376264 | tf_op jit(solution)/shard_map/ppermute | solution.py:402
  81.4 13.3 %collective-permute-start.25 = (f32[896,128]{1,0:T(8,128)S(1)}, f32[896,128]{1,0:T(8,128)S(1)}, u32[]{:S(2)}, u32[]{:S(2)}) collective-permute-start(f32[896,128]{1,0:T(8,128)S(1)} %get-tuple-element.144.refs_0_), channel_id=1, source_target_pairs={{0,2},{1,3},{2,0},{3,1},{4,6},{5,7},{6,4},{7,5},{8,10},{9,11},{10,... | collective-permute-start | bytes 1376264 | tf_op jit(solution)/shard_map/ppermute | solution.py:402
  82.4 2.3 %collective-permute-start.28 = (f32[832,128]{1,0:T(8,128)S(1)}, f32[832,128]{1,0:T(8,128)S(1)}, u32[]{:S(2)}, u32[]{:S(2)}) collective-permute-start(f32[832,128]{1,0:T(8,128)S(1)} %get-tuple-element.145.refs_1_.refs_2_), channel_id=1, source_target_pairs={{0,1},{1,0},{2,3},{3,2},{4,5},{5,4},{6,7},{7,6},{8,9},{9,8},{10,11... | collective-permute-start | bytes 1277960 | tf_op jit(solution)/shard_map/ppermute | solution.py:402
  82.6 12.1 %collective-permute-start.26 = (f32[832,128]{1,0:T(8,128)S(1)}, f32[832,128]{1,0:T(8,128)S(1)}, u32[]{:S(2)}, u32[]{:S(2)}) collective-permute-start(f32[832,128]{1,0:T(8,128)S(1)} %get-tuple-element.145.refs_1_.refs_2_), channel_id=1, source_target_pairs={{0,4},{4,0},{8,12},{12,8},{16,20},{20,16},{24,28},{28,24},{1,5},{5... | collective-permute-start | bytes 1277960 | tf_op jit(solution)/shard_map/ppermute | solution.py:402
  94.6 2.4 %collective-permute-start.29 = (f32[896,128]{1,0:T(8,128)S(1)}, f32[896,128]{1,0:T(8,128)S(1)}, u32[]{:S(2)}, u32[]{:S(2)}) collective-permute-start(f32[896,128]{1,0:T(8,128)S(1)} %collective-permute-done.25.refs_0_), channel_id=1, source_target_pairs={{0,1},{1,0},{2,3},{3,2},{4,5},{5,4},{6,7},{7,6},{8,9},{9,8},{10,11... | collective-permute-start | bytes 1376264 | tf_op jit(solution)/shard_map/ppermute | solution.py:402
  94.6 2.4 %collective-permute-start.30 = (f32[832,128]{1,0:T(8,128)S(1)}, f32[832,128]{1,0:T(8,128)S(1)}, u32[]{:S(2)}, u32[]{:S(2)}) collective-permute-start(f32[832,128]{1,0:T(8,128)S(1)} %collective-permute-done.26.refs_1_), channel_id=1, source_target_pairs={{0,1},{1,0},{2,3},{3,2},{4,5},{5,4},{6,7},{7,6},{8,9},{9,8},{10,11... | collective-permute-start | bytes 1277960 | tf_op jit(solution)/shard_map/ppermute | solution.py:402
  (1 other events, 34.2 us)
